TPU v7x, 256 devices: a whole 4x4x8 slice. The times are simulated.
256 devices in a mesh: gx: 4 (over x_hi, core), gy: 8 (over y, x_lo), gz: 8 (over z).
Axes of the slice: x: 4 (x_hi: 2, x_lo: 2; x = x_hi * 2 + x_lo), y: 4, z: 8, core: 2. Of those that a mesh axis runs over, the one named last changes fastest.
Arguments:
- primal_states: float32 [2, 19, 16, 128, 1024], P(None, None, 'gx', 'gy', 'gz'), as said below
- adjoint_last: float32 [19, 16, 128, 1024], P(None, 'gx', 'gy', 'gz'), may hold values from -6 to 6
- porosity: float32 [16, 128, 1024], P('gx', 'gy', 'gz'), may hold values from 0 to 0.9
- solid_mask: int32 [16, 128, 1024], P('gx', 'gy', 'gz'), may hold values from 0 to 1, as said below
Outputs:
- adjoint_first: float32 [19, 16, 128, 1024], P(None, 'gx', 'gy', 'gz')
- porosity_grad: float32 [16, 128, 1024], P('gx', 'gy', 'gz')
- drag: float32 [], replicated
Inputs may be any that keep to these rules, and one draw needn't show every extreme that they name: `primal_states`: every population is positive. `solid_mask`: every cell on the planes y = 0 and y = 127 is solid; elsewhere cells are solid at random.
All inputs are finite; a program needn't handle non-finite values.
Results may differ from a plain program's by a relative error of at most 0.00013.
Values sent between devices are 32-bit elements; how exact they have to be, the bound alone decides.
A program may use at most 128 MiB of HBM per device.

v0:
```python
import functools

import jax
import jax.numpy as jnp
import numpy as np
from jax import lax
from jax.experimental import pallas as pl
from jax.experimental.pallas import tpu as pltpu
from jax.sharding import PartitionSpec as P

MESH = pl.DeviceIdType.MESH
F32 = jnp.float32

VELOCITY = (
    (0, 0, 0),
    (1, 0, 0),
    (-1, 0, 0),
    (0, 1, 0),
    (0, -1, 0),
    (0, 0, 1),
    (0, 0, -1),
    (1, 1, 0),
    (-1, -1, 0),
    (1, -1, 0),
    (-1, 1, 0),
    (1, 0, 1),
    (-1, 0, -1),
    (1, 0, -1),
    (-1, 0, 1),
    (0, 1, 1),
    (0, -1, -1),
    (0, 1, -1),
    (0, -1, 1),
)
ALONG = tuple(
    {sign: tuple(i for i in range(19) if VELOCITY[i][dim] == sign) for sign in (1, -1)} for dim in range(3)
)
FACES = ((1, 2), (3, 4), (5, 6))
EDGES = (((0, 1), (7, 8), (9, 10)), ((0, 2), (11, 12), (13, 14)), ((1, 2), (15, 16), (17, 18)))


def orthonormal_rows(monomials):
    rows = []
    for column in range(monomials.shape[1]):
        vector = monomials[:, column] * 1.0
        for sweep in range(2):
            for earlier in rows:
                vector = vector - np.dot(earlier, vector) * earlier
        vector = vector / np.sqrt(np.dot(vector, vector))
        rows.append(vector)
    return np.stack(rows)


def coefficients():
    vel = np.array(VELOCITY) * 1.0
    speeds = np.sum(np.abs(vel), axis=1)
    weights = np.where(speeds == 0, 1.0 / 3.0, np.where(speeds == 1, 1.0 / 18.0, 1.0 / 36.0))
    x, y, z = vel[:, 0], vel[:, 1], vel[:, 2]
    columns = [np.ones(19), x, y, z, x * x, y * y, z * z, x * y, x * z, y * z]
    columns += [x * y * y, x * z * z, y * x * x, y * z * z, z * x * x, z * y * y]
    columns += [x * x * y * y, x * x * z * z, y * y * z * z]
    basis = orthonormal_rows(np.stack(columns, axis=1))
    rates = np.array([0.0] * 4 + [1.6] * 6 + [1.2] * 9)
    relax = basis.T @ np.diag(rates) @ basis
    kept = 1.2 * np.eye(19) - relax
    scalar = relax @ weights
    square = relax @ (weights * x * x)
    first = relax @ (weights * x)
    face = (kept[1] + kept[2]) / 2 - kept[0]
    return dict(
        s0=(scalar[0], scalar[1], scalar[7]),
        s1=(first[1], first[7]),
        s2=(square[0], square[3], square[15], square[1] - square[3], square[7] - square[15]),
        s2_mixed=(relax @ (weights * x * y))[7],
        even=(kept[0][0], kept[0][1], kept[0][7]),
        odd=kept[1][1] / 2 - kept[1][2] / 2,
        square=(face[0], face[3], face[15], face[1] - face[3], face[7] - face[15]),
        mixed=(kept[7][7] + kept[8][7] - kept[9][7] - kept[10][7]) / 4,
    )


COEF = {name: tuple(np.asarray(v, np.float64).reshape(-1).tolist()) for name, v in coefficients().items()}


def pair_sums(members):
    face_sum = [members[a] + members[b] for a, b in FACES]
    face_diff = [members[a] - members[b] for a, b in FACES]
    edge = []
    for dims, (a, b), (c, d) in EDGES:
        edge.append((members[a] + members[b], members[a] - members[b], members[c] + members[d], members[c] - members[d]))
    plane = [e[0] + e[2] for e in edge]
    mixed = [e[0] - e[2] for e in edge]
    lean = [(e[1] + e[3], e[1] - e[3]) for e in edge]
    edge_square = [plane[0] + plane[1], plane[0] + plane[2], plane[1] + plane[2]]
    edge_diff = [lean[0][0] + lean[1][0], lean[0][1] + lean[2][0], lean[1][1] + lean[2][1]]
    face_total = face_sum[0] + face_sum[1] + face_sum[2]
    edge_total = plane[0] + plane[1] + plane[2]
    return face_sum, face_diff, edge, mixed, edge_square, edge_diff, face_total, edge_total


def primal_terms(state):
    face_sum, face_diff, edge, mixed, edge_square, edge_diff, face_total, edge_total = pair_sums(state)
    rho = state[0] + face_total + edge_total
    inverse = 1.0 / rho
    flux = [face_diff[a] + edge_diff[a] for a in range(3)]
    vel = [flux[a] * inverse for a in range(3)]
    third = rho * (1.0 / 3.0)
    press = [face_sum[a] + edge_square[a] - third - flux[a] * vel[a] for a in range(3)]
    total = press[0] + press[1] + press[2]
    centre = total * (2.0 / 21.0)
    stress = [0.4 * (press[a] * (1.0 / 6.0) + centre) for a in range(3)]
    shear = [0.1 * (mixed[e] - flux[dims[0]] * vel[dims[1]]) for e, (dims, _, _) in enumerate(EDGES)]
    flat = (stress[0] + stress[1] + stress[2]) * (-10.0 / 19.0)
    usq = vel[0] * vel[0] + vel[1] * vel[1] + vel[2] * vel[2]
    still = rho * (1.0 - 1.5 * usq)
    rest = 1.2 * state[0] + flat - 0.4 * still
    even, odd = [], []
    for a in range(3):
        feq_even = still + (4.5 * flux[a]) * vel[a]
        even.append(0.6 * face_sum[a] + (flat + stress[a]) - (1.2 / 18.0) * feq_even)
        odd.append(-0.4 * face_diff[a] - (3.6 / 18.0) * flux[a])
    for e, (dims, _, _) in enumerate(EDGES):
        p, q = dims
        bend = flat + stress[p] + stress[q]
        for sign, total_pair, diff_pair in ((1, edge[e][0], edge[e][1]), (-1, edge[e][2], edge[e][3])):
            along_flux = flux[p] + flux[q] if sign == 1 else flux[p] - flux[q]
            along_vel = vel[p] + vel[q] if sign == 1 else vel[p] - vel[q]
            feq_even = still + (4.5 * along_flux) * along_vel
            twist = bend + shear[e] if sign == 1 else bend - shear[e]
            even.append(0.6 * total_pair + twist - (1.2 / 36.0) * feq_even)
            odd.append(-0.4 * diff_pair - (3.6 / 36.0) * along_flux)
    return vel, flux[0], [rest] + even + odd


def pull_back(read, vel, blocking):
    c = COEF
    face_sum, face_diff, edge, mixed, edge_square, edge_diff, face_total, edge_total = pair_sums(read)
    rest = read[0]

    def by_class(f):
        return f[0] * rest + f[1] * face_total + f[2] * edge_total

    s0 = by_class(c["s0"])
    s2_flat = by_class(c["s2"][:3])
    s2 = [s2_flat + c["s2"][3] * face_sum[a] + c["s2"][4] * edge_square[a] for a in range(3)]
    shear = [c["s2_mixed"][0] * mixed[e] for e in range(3)]
    xy, xz, yz = shear
    turned = [
        s2[0] * vel[0] + xy * vel[1] + xz * vel[2],
        xy * vel[0] + s2[1] * vel[1] + yz * vel[2],
        xz * vel[0] + yz * vel[1] + s2[2] * vel[2],
    ]
    bend = [3.0 * turned[a] - vel[a] * s0 for a in range(3)]
    density = s0 - 1.5 * (vel[0] * bend[0] + vel[1] * bend[1] + vel[2] * bend[2])
    open_part = 1.0 - blocking
    momentum = []
    for a in range(3):
        s1 = c["s1"][0] * face_diff[a] + c["s1"][1] * edge_diff[a]
        slope = c["odd"][0] * (face_diff[a] + edge_diff[a]) + 3.0 * (s1 + bend[a])
        slope = open_part * slope
        momentum.append(slope + blocking if a == 0 else slope)
    even = open_part * (by_class(c["even"]) + density)
    sq_flat = by_class(c["square"][:3])
    square = [open_part * (sq_flat + c["square"][3] * face_sum[a] + c["square"][4] * edge_square[a]) for a in range(3)]
    cross = [(c["mixed"][0] * open_part) * mixed[e] for e in range(3)]
    keep_sum = 0.6 * blocking - 0.1
    keep_diff = -0.1 - 0.4 * blocking
    out = [None] * 19
    out[0] = (2.0 * keep_sum) * rest + even
    for a, (i, j) in enumerate(FACES):
        half = keep_sum * face_sum[a] + (even + square[a])
        tilt = keep_diff * face_diff[a] + momentum[a]
        out[i], out[j] = half + tilt, half - tilt
    for e, (dims, same, cross_pair) in enumerate(EDGES):
        p, q = dims
        level = even + square[p] + square[q]
        half = keep_sum * edge[e][0] + (level + cross[e])
        tilt = keep_diff * edge[e][1] + (momentum[p] + momentum[q])
        out[same[0]], out[same[1]] = half + tilt, half - tilt
        half = keep_sum * edge[e][2] + (level - cross[e])
        tilt = keep_diff * edge[e][3] + (momentum[p] - momentum[q])
        out[cross_pair[0]], out[cross_pair[1]] = half + tilt, half - tilt
    sums = list(face_sum) + [s for e in edge for s in (e[0], e[2])]
    diffs = list(face_diff) + [d for e in edge for d in (e[1], e[3])]
    return out, [rest] + sums + diffs


def slot(sign):
    return 0 if sign == 1 else 1


def member_at(velocity):
    return VELOCITY.index(velocity)


BODY = 8


def kernel(
    mesh_sizes,
    extent,
    primal,
    adjoint,
    porosity,
    solid,
    out_adjoint,
    out_grad,
    out_drag,
    level_two,
    level_one,
    states,
    porous,
    marks,
    block,
    grad,
    terms,
    result,
    face_send,
    rows_send,
    columns_send,
    face_recv,
    rows_recv,
    columns_recv,
    rows_edge,
    columns_edge,
    drag_row,
    drag_first,
    drag_second,
    load_sem,
    store_sem,
    send_sem,
    recv_sem,
    drag_send_sem,
    drag_recv_sem,
):
    sx, sy, sz = mesh_sizes
    nx, ny, nz = extent
    halves = ny // 8
    body = pl.ds(BODY, ny)
    me = (lax.axis_index("gx"), lax.axis_index("gy"), lax.axis_index("gz"))

    def shifted(offset):
        return tuple(lax.rem(me[d] + mesh_sizes[d] + offset[d], mesh_sizes[d]) for d in range(3))

    faces = [tuple(s if d == dim else 0 for d in range(3)) for dim in range(3) for s in (1, -1)]
    edges = [
        tuple(s if d == p else t if d == q else 0 for d in range(3))
        for p, q in ((0, 2), (0, 1), (1, 2))
        for s in (1, -1)
        for t in (1, -1)
    ]
    around = faces + edges

    pair, core = me[0] // 2, me[0] % 2
    pairs = sx // 2
    first_group = [(c, z) for c in range(2) for z in range(sz) if (c, z) != (0, 0)]
    second_group = [(h, y) for h in range(pairs) for y in range(sy) if (h, y) != (0, 0)]

    def first_partner(c, z):
        return (pair * 2 + lax.rem(core + c, 2), me[1], lax.rem(me[2] + z, sz))

    def second_partner(h, y):
        return (lax.rem(pair + h, pairs) * 2 + core, lax.rem(me[1] + y, sy), me[2])

    barrier = pltpu.get_barrier_semaphore()
    targets = [first_partner(c, z) for c, z in first_group if (c, z) not in ((0, 1), (0, sz - 1))]
    targets += [second_partner(h, y) for h, y in second_group if (h, y) not in ((0, 1), (0, sy - 1))]
    targets += [shifted(offset) for offset in around]
    for target in targets:
        pl.semaphore_signal(barrier, inc=1, device_id=target, device_id_type=MESH)

    loads = [
        pltpu.make_async_copy(adjoint, level_two.at[:, :, body, :], load_sem.at[0]),
        pltpu.make_async_copy(porosity, porous, load_sem.at[1]),
        pltpu.make_async_copy(solid, marks, load_sem.at[2]),
        pltpu.make_async_copy(primal, states, load_sem.at[3]),
    ]
    for load in loads:
        load.start()

    lane = lax.broadcasted_iota(jnp.int32, (8, nz), 1)

    def pack(step, cells):
        for sign in (1, -1):
            at = slot(sign)
            edge_row = BODY if sign == 1 else BODY + ny - 1
            for k, i in enumerate(ALONG[1][sign]):
                for x in range(nx):
                    rows_send[step, at, k * nx + x : k * nx + x + 1, :] = cells[i, x, edge_row : edge_row + 1, :]
            for h in range(halves):
                packed = jnp.zeros((8, nz), F32)
                for k, i in enumerate(ALONG[2][sign]):
                    for x in range(nx):
                        spot = k * nx + x
                        column = cells[i, x, BODY + 8 * h : BODY + 8 * h + 8, :]
                        turn = (spot if sign == 1 else spot + 1) % nz
                        column = pltpu.roll(column, turn, 1) if turn else column
                        packed = jnp.where(lane == spot, column, packed)
                columns_send[step, at, 8 * h : 8 * h + 8, :] = packed

    def messages(step, cells):
        made = {}
        count = 0

        def add(direction, source, target):
            nonlocal count
            back = tuple(-d for d in direction)
            copy = pltpu.make_async_remote_copy(
                src_ref=source,
                dst_ref=target,
                send_sem=send_sem.at[step, count],
                recv_sem=recv_sem.at[step, count],
                device_id=shifted(back),
                device_id_type=MESH,
            )
            made.setdefault(direction, []).append(copy)
            count += 1

        for direction in around:
            dx, dy, dz = direction
            if dx and not dy and not dz:
                near = 0 if dx == 1 else nx - 1
                if step == 0:
                    for k, i in enumerate(ALONG[0][dx]):
                        add(direction, cells.at[i, near, body, :], face_recv.at[step, slot(dx), k, body, :])
                else:
                    add(direction, face_send.at[slot(dx)], face_recv.at[step, slot(dx), :, body, :])
            elif dy and not dx and not dz:
                add(direction, rows_send.at[step, slot(dy)], rows_recv.at[step, slot(dy)])
            elif dz and not dx and not dy:
                add(direction, columns_send.at[step, slot(dz)], columns_recv.at[step, slot(dz), body, :])
            elif not dz:
                row = xy_row(dx, dy)
                source = rows_send.at[step, slot(dy), pl.ds(row // 8 * 8, 8), :]
                add(direction, source, rows_edge.at[step, slot(dx) * 2 + slot(dy)])
            elif not dy:
                source = columns_send.at[step, slot(dz)]
                add(direction, source, columns_edge.at[step, slot(dx) * 2 + slot(dz)])
            else:
                near, far = (0, BODY + ny) if dy == 1 else (ny - 8, BODY - 8)
                source = columns_send.at[step, slot(dz), pl.ds(near, 8), :]
                add(direction, source, columns_recv.at[step, slot(dz), pl.ds(far, 8), :])
        return made

    def xy_row(dx, dy):
        k = ALONG[1][dy].index(member_at((dx, dy, 0)))
        return k * nx + (0 if dx == 1 else nx - 1)

    def halo_row(sign):
        return BODY + ny if sign == 1 else BODY - 1

    def insert_rows(step, cells):
        for sign in (1, -1):
            row = halo_row(sign)
            for k, i in enumerate(ALONG[1][sign]):
                for x in range(nx):
                    if 0 <= x - VELOCITY[i][0] < nx:
                        got = rows_recv[step, slot(sign), k * nx + x : k * nx + x + 1, :]
                        cells[i, x, row : row + 1, :] = got

    def insert_edges(step):
        for dx in (1, -1):
            for dy in (1, -1):
                k = ALONG[0][dx].index(member_at((dx, dy, 0)))
                r = xy_row(dx, dy) % 8
                row = halo_row(dy)
                face_recv[step, slot(dx), k, row : row + 1, :] = rows_edge[step, slot(dx) * 2 + slot(dy), r : r + 1, :]

    def read_cells(step, cells, x, h):
        read = []
        for i, (dx, dy, dz) in enumerate(VELOCITY):
            from_x = x + dx
            outside = not 0 <= from_x < nx
            rows = slice(BODY + 8 * h + dy, BODY + 8 * h + dy + 8)
            if outside:
                value = face_recv[step, slot(dx), ALONG[0][dx].index(i), rows, :]
            else:
                value = cells[i, from_x, rows, :]
            if dz:
                spot = ALONG[2][dz].index(i) * nx + from_x % nx
                if outside:
                    column = columns_edge[step, slot(dx) * 2 + slot(dz), 8 * h : 8 * h + 8, :]
                else:
                    column = columns_recv[step, slot(dz), rows, :]
                last = nz - 1 if dz == 1 else 0
                turn = (last - spot) % nz
                column = pltpu.roll(column, turn, 1) if turn else column
                value = jnp.where(lane == last, column, pltpu.roll(value, nz - 1 if dz == 1 else 1, 1))
            read.append(value)
        return read

    def level(step, cells, x, h):
        rows = slice(8 * h, 8 * h + 8)
        read = read_cells(step, cells, x, h)
        vel = [terms[step, a, x, rows, :] for a in range(3)]
        fresh, weighed = pull_back(read, vel, block[x, rows, :])
        total = grad[x, rows, :]
        for j, value in enumerate(weighed):
            total = total + value * terms[step, 3 + j, x, rows, :]
        grad[x, rows, :] = total
        return fresh

    loads[0].wait()
    pack(0, level_two)
    loads[1].wait()
    loads[2].wait()
    loads[3].wait()
    total = jnp.zeros((8, nz), F32)
    for x in range(nx):
        for h in range(halves):
            rows = slice(8 * h, 8 * h + 8)
            closed = jnp.where(marks[x, rows, :] == 0, porous[x, rows, :], 1.0)
            block[x, rows, :] = closed
            flux = None
            for t in range(2):
                gain = sum(states[t, i, x, rows, :] for i in ALONG[0][1])
                loss = sum(states[t, i, x, rows, :] for i in ALONG[0][-1])
                flux = gain - loss if flux is None else flux + (gain - loss)
            grad[x, rows, :] = flux
            total = total + closed * flux
    drag_row[0] = jnp.sum(total, axis=0, keepdims=True)

    pl.semaphore_wait(barrier, len(targets))

    first = messages(0, level_two)
    for direction in around:
        for copy in first[direction]:
            copy.start()

    mine_first = core * sz + me[2]
    mine_second = pair * sy + me[1]

    def drag_copies(stage, source, target, mine, group, partner, base):
        return [
            pltpu.make_async_remote_copy(
                src_ref=source,
                dst_ref=target.at[mine],
                send_sem=drag_send_sem.at[base + n],
                recv_sem=drag_recv_sem.at[base + n],
                device_id=partner(*offset),
                device_id_type=MESH,
            )
            for n, offset in enumerate(group)
        ]

    gather_first = drag_copies(0, drag_row.at[0], drag_first, mine_first, first_group, first_partner, 0)
    for copy in gather_first:
        copy.start()
    drag_first[mine_first] = drag_row[0]

    for step, t in ((0, 1), (1, 0)):
        for x in range(nx):
            for h in range(halves):
                rows = slice(8 * h, 8 * h + 8)
                vel, _, weights = primal_terms([states[t, i, x, rows, :] for i in range(19)])
                for j, value in enumerate(vel + weights):
                    terms[step, j, x, rows, :] = value

    for direction in around:
        for copy in first[direction]:
            copy.wait_recv()
    insert_rows(0, level_two)
    insert_edges(0)

    second = messages(1, level_one)

    def first_level(x):
        for h in range(halves):
            fresh = level(0, level_two, x, h)
            for i in range(19):
                level_one[i, x, BODY + 8 * h : BODY + 8 * h + 8, :] = fresh[i]
            for sign, near in ((1, 0), (-1, nx - 1)):
                if x == near:
                    for k, i in enumerate(ALONG[0][sign]):
                        face_send[slot(sign), k, 8 * h : 8 * h + 8, :] = fresh[i]

    first_level(0)
    first_level(nx - 1)
    for direction in faces[:2]:
        for copy in second[direction]:
            copy.start()
    for x in range(1, nx - 1):
        first_level(x)
    pack(1, level_one)
    for direction in around[2:]:
        for copy in second[direction]:
            copy.start()

    for copy in gather_first:
        copy.wait_recv()
    drag_row[1] = jnp.sum(drag_first[...], axis=0)
    gather_second = drag_copies(1, drag_row.at[1], drag_second, mine_second, second_group, second_partner, len(first_group))
    for copy in gather_second:
        copy.start()
    drag_second[mine_second] = drag_row[1]

    def second_level(x):
        for h in range(halves):
            rows = slice(8 * h, 8 * h + 8)
            fresh = level(1, level_one, x, h)
            for i in range(19):
                result[i, x, rows, :] = fresh[i]
        store = pltpu.make_async_copy(result.at[:, x], out_adjoint.at[:, x], store_sem.at[x])
        store.start()
        return store

    stores = []
    late = [d for d in around if d[0]]
    for direction in around:
        if direction not in late:
            for copy in second[direction]:
                copy.wait_recv()
    insert_rows(1, level_one)
    for x in range(1, nx - 1):
        stores.append(second_level(x))
    for direction in late:
        for copy in second[direction]:
            copy.wait_recv()
    insert_edges(1)
    for x in (0, nx - 1):
        stores.append(second_level(x))

    for x in range(nx):
        out_grad[x] = jnp.where(marks[x] == 0, grad[x], 0.0)

    for copy in gather_second:
        copy.wait_recv()
    everyone = jnp.sum(jnp.sum(drag_second[...], axis=0)) * (1.0 / (nx * ny * nz * sx * sy * sz))
    out_drag[0, 0] = everyone

    for store in stores:
        store.wait()
    for sent in (first, second):
        for direction in around:
            for copy in sent[direction]:
                copy.wait_send()
    for copy in gather_first + gather_second:
        copy.wait_send()


def solution(mesh):
    sizes = tuple(mesh.shape[name] for name in ("gx", "gy", "gz"))

    def body(primal_states, adjoint_last, porosity, solid_mask):
        nx, ny, nz = porosity.shape
        padded = ny + 16
        row_tiles = -(-5 * nx // 8) * 8
        copies = 26
        links = (2 * sizes[2] - 1) + (sizes[0] // 2 * sizes[1] - 1)
        hbm = pl.BlockSpec(memory_space=pl.ANY)
        adjoint, gradient, drag = pl.pallas_call(
            functools.partial(kernel, sizes, (nx, ny, nz)),
            name="adjoint_window",
            out_shape=(
                jax.ShapeDtypeStruct((19, nx, ny, nz), F32),
                jax.ShapeDtypeStruct((nx, ny, nz), F32),
                jax.ShapeDtypeStruct((1, 1), F32),
            ),
            in_specs=[hbm] * 4,
            out_specs=(
                hbm,
                pl.BlockSpec(memory_space=pltpu.VMEM),
                pl.BlockSpec(memory_space=pltpu.SMEM),
            ),
            scratch_shapes=[
                pltpu.VMEM((19, nx, padded, nz), F32),
                pltpu.VMEM((19, nx, padded, nz), F32),
                pltpu.VMEM((2, 19, nx, ny, nz), F32),
                pltpu.VMEM((nx, ny, nz), F32),
                pltpu.VMEM((nx, ny, nz), jnp.int32),
                pltpu.VMEM((nx, ny, nz), F32),
                pltpu.VMEM((nx, ny, nz), F32),
                pltpu.VMEM((2, 22, nx, ny, nz), F32),
                pltpu.VMEM((19, nx, ny, nz), F32),
                pltpu.VMEM((2, 5, ny, nz), F32),
                pltpu.VMEM((2, 2, row_tiles, nz), F32),
                pltpu.VMEM((2, 2, ny, nz), F32),
                pltpu.VMEM((2, 2, 5, padded, nz), F32),
                pltpu.VMEM((2, 2, row_tiles, nz), F32),
                pltpu.VMEM((2, 2, padded, nz), F32),
                pltpu.VMEM((2, 4, 8, nz), F32),
                pltpu.VMEM((2, 4, ny, nz), F32),
                pltpu.VMEM((2, 1, nz), F32),
                pltpu.VMEM((2 * sizes[2], 1, nz), F32),
                pltpu.VMEM((sizes[0] // 2 * sizes[1], 1, nz), F32),
                pltpu.SemaphoreType.DMA((4,)),
                pltpu.SemaphoreType.DMA((nx,)),
                pltpu.SemaphoreType.DMA((2, copies)),
                pltpu.SemaphoreType.DMA((2, copies)),
                pltpu.SemaphoreType.DMA((links,)),
                pltpu.SemaphoreType.DMA((links,)),
            ],
            compiler_params=pltpu.CompilerParams(collective_id=0, has_side_effects=True),
        )(primal_states, adjoint_last, porosity, solid_mask)
        return adjoint, gradient, drag.reshape(())

    return jax.shard_map(
        body,
        mesh=mesh,
        in_specs=(
            P(None, None, "gx", "gy", "gz"),
            P(None, "gx", "gy", "gz"),
            P("gx", "gy", "gz"),
            P("gx", "gy", "gz"),
        ),
        out_specs=(P(None, "gx", "gy", "gz"), P("gx", "gy", "gz"), P()),
        check_vma=False,
    )
```

profile of v0, /device:TPU:1, one launch (start us, length us, event | category | flops | bytes accessed | tf_op | source)
XLA Modules:
  0.0 29.8 jit_solution(15354108023669017200)
XLA Ops:
  0.6 24.8 %adjoint_window.1 = (f32[19,4,16,128]{3,2,1,0:T(8,128)}, f32[4,16,128]{2,1,0:T(8,128)}, f32[1,1]{1,0:T(1,128)}) custom-call(f32[2,19,4,16,128]{4,3,2,1,0:T(8,128)} %primal.1, f32[19,4,16,128]{3,2,1,0:T(8,128)} %adjoint.1, f32[4,16,128]{2,1,0:T(8,128)} %porosity.1, s32[4,16,128]{2,1,0:T(8,128)} %solid.1), custom_call_target="tpu_custom_call" | custom-call | tf_op jit(solution)/shard_map/adjoint_window/pallas_call | solution.py:551
  25.4 0.0 copy-start
  25.4 2.0 %copy.10 = f32[19,4,16,128]{3,2,1,0:T(8,128)} copy(f32[19,4,16,128]{3,2,1,0:T(8,128)} %get-tuple-element.12) | data formatting | bytes 1245184
  27.4 0.0 copy-done
  27.4 0.6 %copy.11 = f32[4,16,128]{2,1,0:T(8,128)} copy(f32[4,16,128]{2,1,0:T(8,128)S(1)} %copy-done) | data formatting | bytes 65536
Async XLA Ops:
  25.4 2.0 %copy-start = (f32[4,16,128]{2,1,0:T(8,128)S(1)}, f32[4,16,128]{2,1,0:T(8,128)}, u32[]{:S(2)}) copy-start(f32[4,16,128]{2,1,0:T(8,128)} %get-tuple-element.13) | copy-start | bytes 98308
where the time goes:
time: 29.9 us; the launch traced here: 29.8 us
  Pallas kernels  24.8 us (83%)
  local copies, waits for them, and re-layouts  2.58 us (9%)
  between operations  2.41 us (8%)
    pallas_call x1, Pallas kernels, body(): pl.pallas_call(functools.partial(kernel, sizes, (nx, ny, nz)), name='adjo...  24.8 us
    unnamed x4, local copies, waits for them, and re-layouts  2.58 us

commit v1 on v0

--- a/solution.py
+++ b/solution.py
@@ -212,9 +212,8 @@
     porous,
     marks,
     block,
-    grad,
     terms,
-    result,
+    sums,
     face_send,
     rows_send,
     columns_send,
@@ -224,32 +223,51 @@
     rows_edge,
     columns_edge,
     drag_row,
-    drag_first,
-    drag_second,
+    drag_slots,
+    meter,
     load_sem,
-    store_sem,
     send_sem,
     recv_sem,
-    drag_send_sem,
-    drag_recv_sem,
+    drag_sem,
 ):
     sx, sy, sz = mesh_sizes
     nx, ny, nz = extent
     halves = ny // 8
     body = pl.ds(BODY, ny)
+    inner = tuple(range(1, nx - 1))
+    outer = (0, nx - 1)
     me = (lax.axis_index("gx"), lax.axis_index("gy"), lax.axis_index("gz"))
+    loads = [
+        pltpu.make_async_copy(adjoint, level_two.at[:, :, body, :], load_sem.at[0]),
+        pltpu.make_async_copy(primal, states, load_sem.at[1]),
+        pltpu.make_async_copy(porosity, porous, load_sem.at[2]),
+        pltpu.make_async_copy(solid, marks, load_sem.at[3]),
+    ]
+    for load in loads:
+        load.start()
+
+    stepped = tuple(
+        {
+            0: me[d],
+            1: jnp.where(me[d] == mesh_sizes[d] - 1, 0, me[d] + 1),
+            -1: jnp.where(me[d] == 0, mesh_sizes[d] - 1, me[d] - 1),
+        }
+        for d in range(3)
+    )
 
     def shifted(offset):
-        return tuple(lax.rem(me[d] + mesh_sizes[d] + offset[d], mesh_sizes[d]) for d in range(3))
+        return tuple(stepped[d][offset[d]] for d in range(3))
 
     faces = [tuple(s if d == dim else 0 for d in range(3)) for dim in range(3) for s in (1, -1)]
     edges = [
         tuple(s if d == p else t if d == q else 0 for d in range(3))
-        for p, q in ((0, 2), (0, 1), (1, 2))
+        for p, q in ((0, 2), (1, 2), (0, 1))
         for s in (1, -1)
         for t in (1, -1)
     ]
-    around = faces + edges
+    around = edges + faces
+    near_part = [d for d in around if not d[0]]
+    side_part = [d for d in around if d[0]]
 
     pair, core = me[0] // 2, me[0] % 2
     pairs = sx // 2
@@ -269,78 +287,80 @@
     for target in targets:
         pl.semaphore_signal(barrier, inc=1, device_id=target, device_id_type=MESH)
 
-    loads = [
-        pltpu.make_async_copy(adjoint, level_two.at[:, :, body, :], load_sem.at[0]),
-        pltpu.make_async_copy(porosity, porous, load_sem.at[1]),
-        pltpu.make_async_copy(solid, marks, load_sem.at[2]),
-        pltpu.make_async_copy(primal, states, load_sem.at[3]),
-    ]
-    for load in loads:
-        load.start()
+    for sign in (1, -1):
+        for k, i in enumerate(ALONG[0][sign]):
+            source = adjoint.at[i, 0 if sign == 1 else nx - 1]
+            pltpu.make_async_copy(source, face_send.at[0, slot(sign), k], load_sem.at[4]).start()
 
     lane = lax.broadcasted_iota(jnp.int32, (8, nz), 1)
 
-    def pack(step, cells):
+    def pack(step, cells, planes, again):
         for sign in (1, -1):
             at = slot(sign)
-            edge_row = BODY if sign == 1 else BODY + ny - 1
-            for k, i in enumerate(ALONG[1][sign]):
-                for x in range(nx):
-                    rows_send[step, at, k * nx + x : k * nx + x + 1, :] = cells[i, x, edge_row : edge_row + 1, :]
             for h in range(halves):
-                packed = jnp.zeros((8, nz), F32)
+                rows = slice(8 * h, 8 * h + 8)
+                packed = columns_send[step, at, rows, :] if again else jnp.zeros((8, nz), F32)
                 for k, i in enumerate(ALONG[2][sign]):
-                    for x in range(nx):
+                    for x in planes:
                         spot = k * nx + x
                         column = cells[i, x, BODY + 8 * h : BODY + 8 * h + 8, :]
                         turn = (spot if sign == 1 else spot + 1) % nz
                         column = pltpu.roll(column, turn, 1) if turn else column
                         packed = jnp.where(lane == spot, column, packed)
-                columns_send[step, at, 8 * h : 8 * h + 8, :] = packed
-
-    def messages(step, cells):
-        made = {}
-        count = 0
-
-        def add(direction, source, target):
-            nonlocal count
-            back = tuple(-d for d in direction)
-            copy = pltpu.make_async_remote_copy(
-                src_ref=source,
-                dst_ref=target,
-                send_sem=send_sem.at[step, count],
-                recv_sem=recv_sem.at[step, count],
-                device_id=shifted(back),
-                device_id_type=MESH,
-            )
-            made.setdefault(direction, []).append(copy)
-            count += 1
-
-        for direction in around:
-            dx, dy, dz = direction
-            if dx and not dy and not dz:
-                near = 0 if dx == 1 else nx - 1
-                if step == 0:
-                    for k, i in enumerate(ALONG[0][dx]):
-                        add(direction, cells.at[i, near, body, :], face_recv.at[step, slot(dx), k, body, :])
-                else:
-                    add(direction, face_send.at[slot(dx)], face_recv.at[step, slot(dx), :, body, :])
-            elif dy and not dx and not dz:
-                add(direction, rows_send.at[step, slot(dy)], rows_recv.at[step, slot(dy)])
-            elif dz and not dx and not dy:
-                add(direction, columns_send.at[step, slot(dz)], columns_recv.at[step, slot(dz), body, :])
-            elif not dz:
-                row = xy_row(dx, dy)
-                source = rows_send.at[step, slot(dy), pl.ds(row // 8 * 8, 8), :]
-                add(direction, source, rows_edge.at[step, slot(dx) * 2 + slot(dy)])
-            elif not dy:
-                source = columns_send.at[step, slot(dz)]
-                add(direction, source, columns_edge.at[step, slot(dx) * 2 + slot(dz)])
-            else:
-                near, far = (0, BODY + ny) if dy == 1 else (ny - 8, BODY - 8)
-                source = columns_send.at[step, slot(dz), pl.ds(near, 8), :]
-                add(direction, source, columns_recv.at[step, slot(dz), pl.ds(far, 8), :])
-        return made
+                columns_send[step, at, rows, :] = packed
+            edge_row = BODY if sign == 1 else BODY + ny - 1
+            for k, i in enumerate(ALONG[1][sign]):
+                for x in planes:
+                    rows_send[step, at, k * nx + x : k * nx + x + 1, :] = cells[i, x, edge_row : edge_row + 1, :]
+
+    def message(step, direction):
+        dx, dy, dz = direction
+        if dx and not dy and not dz:
+            source = face_send.at[step, slot(dx)]
+            target = face_recv.at[step, slot(dx), :, body, :]
+            tiles = 5 * halves
+        elif dy and not dx and not dz:
+            source = rows_send.at[step, slot(dy)]
+            target = rows_recv.at[step, slot(dy)]
+            tiles = rows_send.shape[2] // 8
+        elif dz and not dx and not dy:
+            source = columns_send.at[step, slot(dz)]
+            target = columns_recv.at[step, slot(dz), body, :]
+            tiles = halves
+        elif not dz:
+            source = rows_send.at[step, slot(dy), pl.ds(xy_row(dx, dy) // 8 * 8, 8), :]
+            target = rows_edge.at[step, slot(dx) * 2 + slot(dy)]
+            tiles = 1
+        elif not dy:
+            source = columns_send.at[step, slot(dz)]
+            target = columns_edge.at[step, slot(dx) * 2 + slot(dz)]
+            tiles = halves
+        else:
+            near, far = (0, BODY + ny) if dy == 1 else (ny - 8, BODY - 8)
+            source = columns_send.at[step, slot(dz), pl.ds(near, 8), :]
+            target = columns_recv.at[step, slot(dz), pl.ds(far, 8), :]
+            tiles = 1
+        copy = pltpu.make_async_remote_copy(
+            src_ref=source,
+            dst_ref=target,
+            send_sem=send_sem.at[0],
+            recv_sem=recv_sem.at[step, 1 if dx else 0],
+            device_id=shifted(tuple(-d for d in direction)),
+            device_id_type=MESH,
+        )
+        return copy, tiles
+
+    def send(step, directions):
+        total = 0
+        for direction in directions:
+            copy, tiles = message(step, direction)
+            copy.start()
+            total += tiles
+        return total
+
+    def await_tiles(tiles, semaphore):
+        whole = meter.at[pl.ds(0, tiles)]
+        pltpu.make_async_copy(whole, whole, semaphore).wait()
 
     def xy_row(dx, dy):
         k = ALONG[1][dy].index(member_at((dx, dy, 0)))
@@ -393,18 +413,18 @@
         rows = slice(8 * h, 8 * h + 8)
         read = read_cells(step, cells, x, h)
         vel = [terms[step, a, x, rows, :] for a in range(3)]
-        fresh, weighed = pull_back(read, vel, block[x, rows, :])
-        total = grad[x, rows, :]
-        for j, value in enumerate(weighed):
-            total = total + value * terms[step, 3 + j, x, rows, :]
-        grad[x, rows, :] = total
-        return fresh
+        return pull_back(read, vel, block[x, rows, :])
+
+    def gradient(step, weighed, x, rows):
+        total = weighed[0] * terms[step, 3, x, rows, :]
+        for j in range(1, 19):
+            total = total + weighed[j] * terms[step, 3 + j, x, rows, :]
+        return total
 
     loads[0].wait()
-    pack(0, level_two)
-    loads[1].wait()
-    loads[2].wait()
-    loads[3].wait()
+    pack(0, level_two, range(nx), False)
+    for load in loads[1:]:
+        load.wait()
     total = jnp.zeros((8, nz), F32)
     for x in range(nx):
         for h in range(halves):
@@ -416,37 +436,40 @@
                 gain = sum(states[t, i, x, rows, :] for i in ALONG[0][1])
                 loss = sum(states[t, i, x, rows, :] for i in ALONG[0][-1])
                 flux = gain - loss if flux is None else flux + (gain - loss)
-            grad[x, rows, :] = flux
+            out_grad[x, rows, :] = flux
             total = total + closed * flux
     drag_row[0] = jnp.sum(total, axis=0, keepdims=True)
+    faces_in = face_send.at[0]
+    pltpu.make_async_copy(faces_in, faces_in, load_sem.at[4]).wait()
 
     pl.semaphore_wait(barrier, len(targets))
 
-    first = messages(0, level_two)
-    for direction in around:
-        for copy in first[direction]:
-            copy.start()
+    sent = send(0, around)
+    near_tiles = sum(message_tiles(d, nx, halves) for d in near_part)
+    side_tiles = sum(message_tiles(d, nx, halves) for d in side_part)
 
     mine_first = core * sz + me[2]
     mine_second = pair * sy + me[1]
-
-    def drag_copies(stage, source, target, mine, group, partner, base):
-        return [
+    drag_first = drag_slots.at[pl.ds(0, 2 * sz)]
+    drag_second = drag_slots.at[pl.ds(2 * sz, pairs * sy)]
+
+    def drag_send(stage, target, mine, group, partner):
+        target[mine] = drag_row[stage]
+        for offset in group:
             pltpu.make_async_remote_copy(
-                src_ref=source,
+                src_ref=drag_row.at[stage],
                 dst_ref=target.at[mine],
-                send_sem=drag_send_sem.at[base + n],
-                recv_sem=drag_recv_sem.at[base + n],
+                send_sem=drag_sem.at[2],
+                recv_sem=drag_sem.at[stage],
                 device_id=partner(*offset),
                 device_id_type=MESH,
-            )
-            for n, offset in enumerate(group)
-        ]
-
-    gather_first = drag_copies(0, drag_row.at[0], drag_first, mine_first, first_group, first_partner, 0)
-    for copy in gather_first:
-        copy.start()
-    drag_first[mine_first] = drag_row[0]
+            ).start()
+
+    def await_rows(target, count, semaphore):
+        whole = target.at[pl.ds(0, count)]
+        pltpu.make_async_copy(whole, whole, semaphore).wait()
+
+    drag_send(0, drag_first, mine_first, first_group, first_partner)
 
     for step, t in ((0, 1), (1, 0)):
         for x in range(nx):
@@ -456,86 +479,86 @@
                 for j, value in enumerate(vel + weights):
                     terms[step, j, x, rows, :] = value
 
-    for direction in around:
-        for copy in first[direction]:
-            copy.wait_recv()
-    insert_rows(0, level_two)
-    insert_edges(0)
-
-    second = messages(1, level_one)
-
     def first_level(x):
         for h in range(halves):
-            fresh = level(0, level_two, x, h)
+            fresh, weighed = level(0, level_two, x, h)
+            rows = slice(8 * h, 8 * h + 8)
             for i in range(19):
                 level_one[i, x, BODY + 8 * h : BODY + 8 * h + 8, :] = fresh[i]
+                sums[i, x, rows, :] = weighed[i]
             for sign, near in ((1, 0), (-1, nx - 1)):
                 if x == near:
                     for k, i in enumerate(ALONG[0][sign]):
-                        face_send[slot(sign), k, 8 * h : 8 * h + 8, :] = fresh[i]
-
-    first_level(0)
-    first_level(nx - 1)
-    for direction in faces[:2]:
-        for copy in second[direction]:
-            copy.start()
-    for x in range(1, nx - 1):
+                        face_send[1, slot(sign), k, rows, :] = fresh[i]
+
+    await_tiles(near_tiles, recv_sem.at[0, 0])
+    insert_rows(0, level_two)
+    for x in inner:
         first_level(x)
-    pack(1, level_one)
-    for direction in around[2:]:
-        for copy in second[direction]:
-            copy.start()
-
-    for copy in gather_first:
-        copy.wait_recv()
+    pack(1, level_one, inner, False)
+    await_tiles(side_tiles, recv_sem.at[0, 1])
+    insert_edges(0)
+    for x in outer:
+        first_level(x)
+    pack(1, level_one, outer, True)
+    sent += send(1, around)
+
+    await_rows(drag_first, len(first_group), drag_sem.at[0])
     drag_row[1] = jnp.sum(drag_first[...], axis=0)
-    gather_second = drag_copies(1, drag_row.at[1], drag_second, mine_second, second_group, second_partner, len(first_group))
-    for copy in gather_second:
-        copy.start()
-    drag_second[mine_second] = drag_row[1]
+    drag_send(1, drag_second, mine_second, second_group, second_partner)
+
+    for x in range(nx):
+        for h in range(halves):
+            rows = slice(8 * h, 8 * h + 8)
+            weighed = [sums[j, x, rows, :] for j in range(19)]
+            out_grad[x, rows, :] = out_grad[x, rows, :] + gradient(0, weighed, x, rows)
 
     def second_level(x):
         for h in range(halves):
             rows = slice(8 * h, 8 * h + 8)
-            fresh = level(1, level_one, x, h)
+            fresh, weighed = level(1, level_one, x, h)
             for i in range(19):
-                result[i, x, rows, :] = fresh[i]
-        store = pltpu.make_async_copy(result.at[:, x], out_adjoint.at[:, x], store_sem.at[x])
-        store.start()
-        return store
-
-    stores = []
-    late = [d for d in around if d[0]]
-    for direction in around:
-        if direction not in late:
-            for copy in second[direction]:
-                copy.wait_recv()
+                out_adjoint[i, x, rows, :] = fresh[i]
+            total = out_grad[x, rows, :] + gradient(1, weighed, x, rows)
+            out_grad[x, rows, :] = jnp.where(marks[x, rows, :] == 0, total, 0.0)
+
+    await_tiles(near_tiles, recv_sem.at[1, 0])
     insert_rows(1, level_one)
-    for x in range(1, nx - 1):
-        stores.append(second_level(x))
-    for direction in late:
-        for copy in second[direction]:
-            copy.wait_recv()
+    for x in inner:
+        second_level(x)
+    await_tiles(side_tiles, recv_sem.at[1, 1])
     insert_edges(1)
-    for x in (0, nx - 1):
-        stores.append(second_level(x))
-
-    for x in range(nx):
-        out_grad[x] = jnp.where(marks[x] == 0, grad[x], 0.0)
-
-    for copy in gather_second:
-        copy.wait_recv()
-    everyone = jnp.sum(jnp.sum(drag_second[...], axis=0)) * (1.0 / (nx * ny * nz * sx * sy * sz))
-    out_drag[0, 0] = everyone
-
-    for store in stores:
-        store.wait()
-    for sent in (first, second):
-        for direction in around:
-            for copy in sent[direction]:
-                copy.wait_send()
-    for copy in gather_first + gather_second:
-        copy.wait_send()
+    for x in outer:
+        second_level(x)
+
+    await_rows(drag_second, len(second_group), drag_sem.at[1])
+    everyone = jnp.sum(drag_second[...], axis=0)
+    cells_in_all = nx * ny * nz * sx * sy * sz
+    out_drag[...] = jnp.broadcast_to(everyone * (1.0 / cells_in_all), (8, nz))
+
+    await_tiles(sent, send_sem.at[0])
+    await_rows(drag_slots, len(first_group) + len(second_group), drag_sem.at[2])
+
+
+def message_tiles(direction, nx, halves):
+    dx, dy, dz = (d != 0 for d in direction)
+    if dx and not dy and not dz:
+        return 5 * halves
+    if dy and not dx and not dz:
+        return -(-5 * nx // 8)
+    return halves if dz and not dy else 1
+
+
+def put_out(adjoint, gradient, drag, out_adjoint, out_gradient, out_drag, sem):
+    copies = [
+        pltpu.make_async_copy(adjoint, out_adjoint, sem.at[0]),
+        pltpu.make_async_copy(gradient, out_gradient, sem.at[1]),
+    ]
+    for copy in copies:
+        copy.start()
+    out_drag[...] = jnp.sum(drag[0:1, :], axis=1, keepdims=True)
+    for copy in copies:
+        copy.wait()
 
 
 def solution(mesh):
@@ -545,23 +568,22 @@
         nx, ny, nz = porosity.shape
         padded = ny + 16
         row_tiles = -(-5 * nx // 8) * 8
-        copies = 26
-        links = (2 * sizes[2] - 1) + (sizes[0] // 2 * sizes[1] - 1)
-        hbm = pl.BlockSpec(memory_space=pl.ANY)
-        adjoint, gradient, drag = pl.pallas_call(
+        hbm = pl.BlockSpec(memory_space=pltpu.HBM)
+        vmem = pl.BlockSpec(memory_space=pltpu.VMEM)
+        arguments = [
+            pltpu.with_memory_space_constraint(v, pltpu.HBM)
+            for v in (primal_states, adjoint_last, porosity, solid_mask)
+        ]
+        results = pl.pallas_call(
             functools.partial(kernel, sizes, (nx, ny, nz)),
             name="adjoint_window",
             out_shape=(
-                jax.ShapeDtypeStruct((19, nx, ny, nz), F32),
-                jax.ShapeDtypeStruct((nx, ny, nz), F32),
-                jax.ShapeDtypeStruct((1, 1), F32),
+                pltpu.VMEM((19, nx, ny, nz), F32),
+                pltpu.VMEM((nx, ny, nz), F32),
+                pltpu.VMEM((8, nz), F32),
             ),
             in_specs=[hbm] * 4,
-            out_specs=(
-                hbm,
-                pl.BlockSpec(memory_space=pltpu.VMEM),
-                pl.BlockSpec(memory_space=pltpu.SMEM),
-            ),
+            out_specs=(vmem, vmem, vmem),
             scratch_shapes=[
                 pltpu.VMEM((19, nx, padded, nz), F32),
                 pltpu.VMEM((19, nx, padded, nz), F32),
@@ -569,10 +591,9 @@
                 pltpu.VMEM((nx, ny, nz), F32),
                 pltpu.VMEM((nx, ny, nz), jnp.int32),
                 pltpu.VMEM((nx, ny, nz), F32),
-                pltpu.VMEM((nx, ny, nz), F32),
                 pltpu.VMEM((2, 22, nx, ny, nz), F32),
                 pltpu.VMEM((19, nx, ny, nz), F32),
-                pltpu.VMEM((2, 5, ny, nz), F32),
+                pltpu.VMEM((2, 2, 5, ny, nz), F32),
                 pltpu.VMEM((2, 2, row_tiles, nz), F32),
                 pltpu.VMEM((2, 2, ny, nz), F32),
                 pltpu.VMEM((2, 2, 5, padded, nz), F32),
@@ -581,17 +602,30 @@
                 pltpu.VMEM((2, 4, 8, nz), F32),
                 pltpu.VMEM((2, 4, ny, nz), F32),
                 pltpu.VMEM((2, 1, nz), F32),
-                pltpu.VMEM((2 * sizes[2], 1, nz), F32),
-                pltpu.VMEM((sizes[0] // 2 * sizes[1], 1, nz), F32),
-                pltpu.SemaphoreType.DMA((4,)),
-                pltpu.SemaphoreType.DMA((nx,)),
-                pltpu.SemaphoreType.DMA((2, copies)),
-                pltpu.SemaphoreType.DMA((2, copies)),
-                pltpu.SemaphoreType.DMA((links,)),
-                pltpu.SemaphoreType.DMA((links,)),
+                pltpu.VMEM((2 * sizes[2] + sizes[0] // 2 * sizes[1], 1, nz), F32),
+                pltpu.VMEM((128, 8, nz), F32),
+                pltpu.SemaphoreType.DMA((5,)),
+                pltpu.SemaphoreType.DMA((1,)),
+                pltpu.SemaphoreType.DMA((2, 2)),
+                pltpu.SemaphoreType.DMA((3,)),
             ],
-            compiler_params=pltpu.CompilerParams(collective_id=0, has_side_effects=True),
-        )(primal_states, adjoint_last, porosity, solid_mask)
+            compiler_params=pltpu.CompilerParams(
+                collective_id=0, has_side_effects=True, vmem_limit_bytes=16 << 20
+            ),
+        )(*arguments)
+        adjoint, gradient, drag = pl.pallas_call(
+            put_out,
+            name="put_out",
+            out_shape=(
+                jax.ShapeDtypeStruct((19, nx, ny, nz), F32),
+                jax.ShapeDtypeStruct((nx, ny, nz), F32),
+                jax.ShapeDtypeStruct((1, 1), F32),
+            ),
+            in_specs=[vmem] * 3,
+            out_specs=(hbm, hbm, vmem),
+            scratch_shapes=[pltpu.SemaphoreType.DMA((2,))],
+            compiler_params=pltpu.CompilerParams(vmem_limit_bytes=1 << 20),
+        )(*results)
         return adjoint, gradient, drag.reshape(())
 
     return jax.shard_map(

time: 29.9 us -> 24.2 us (0.81)
  local copies, waits for them, and re-layouts: 2.58 us -> 0 us
  between operations: 2.41 us -> 0.64 us
  Pallas kernels: 24.8 us -> 23.4 us
    pallas_call x1, Pallas kernels: 24.8 us -> 22 us  [body(): pl.pallas_call(functools.partial(kernel, sizes, (nx, ny, nz)), name='adjo...]
    unnamed x4 -> x0, local copies, waits for them, and re-layouts: 2.58 us -> none
    pallas_call x0 -> x1, Pallas kernels: none -> 1.36 us  [body(): pl.pallas_call(put_out, name='put_out', out_shape=(jax.ShapeDtypeStruct((...]
where the time goes in v1:
time: 24.2 us; the launch traced here: 24 us
  Pallas kernels  23.4 us (97%)
  between operations  0.64 us (3%)
    pallas_call x1, Pallas kernels, body(): pl.pallas_call(functools.partial(kernel, sizes, (nx, ny, nz)), name='adjo...  22 us
    pallas_call x1, Pallas kernels, body(): pl.pallas_call(put_out, name='put_out', out_shape=(jax.ShapeDtypeStruct((...  1.36 us

profile of v1, /device:TPU:1, one launch (start us, length us, event | category | flops | bytes accessed | tf_op | source)
XLA Modules:
  0.0 24.0 jit_solution(3737524363592912686)
XLA Ops:
  0.6 22.0 %adjoint_window.1 = (f32[19,4,16,128]{3,2,1,0:T(8,128)S(1)}, f32[4,16,128]{2,1,0:T(8,128)S(1)}, f32[8,128]{1,0:T(8,128)S(1)}) custom-call(f32[2,19,4,16,128]{4,3,2,1,0:T(8,128)} %primal.1, f32[19,4,16,128]{3,2,1,0:T(8,128)} %adjoint.1, f32[4,16,128]{2,1,0:T(8,128)} %porosity.1, s32[4,16,128]{2,1,0:T(8,128)} %solid.1), custom_call_target="tpu_custom_call" | custom-call | tf_op jit(solution)/shard_map/adjoint_window/pallas_call | solution.py:577
  22.7 1.4 %put_out.1 = (f32[19,4,16,128]{3,2,1,0:T(8,128)}, f32[4,16,128]{2,1,0:T(8,128)}, f32[1,1]{1,0:T(1,128)}) custom-call(f32[19,4,16,128]{3,2,1,0:T(8,128)S(1)} %get-tuple-element.9.adjoint, f32[4,16,128]{2,1,0:T(8,128)S(1)} %get-tuple-element.10.gradient, f32[8,128]{1,0:T(8,128)S(1)} %get-tuple-element.11.drag), custom_call_target="tpu_custom_call" | custom-call | tf_op jit(solution)/shard_map/put_out/pallas_call | solution.py:616

commit v2 on v1

--- a/solution.py
+++ b/solution.py
@@ -132,48 +132,61 @@
     return vel, flux[0], [rest] + even + odd
 
 
-def pull_back(read, vel, blocking):
+FACTORS = 6
+
+
+def blocking_factors(blocking):
+    open_part = 1.0 - blocking
+    return [
+        blocking,
+        open_part,
+        COEF["square"][3] * open_part,
+        COEF["mixed"][0] * open_part,
+        0.6 * blocking - 0.1,
+        -0.1 - 0.4 * blocking,
+    ]
+
+
+def pull_back(read, vel, factors):
     c = COEF
+    blocking, open_part, open_square, open_mixed, keep_sum, keep_diff = factors
     face_sum, face_diff, edge, mixed, edge_square, edge_diff, face_total, edge_total = pair_sums(read)
     rest = read[0]
+    twice = face_total + 2.0 * edge_total
+    count = rest + (face_total + edge_total)
 
     def by_class(f):
-        return f[0] * rest + f[1] * face_total + f[2] * edge_total
-
-    s0 = by_class(c["s0"])
-    s2_flat = by_class(c["s2"][:3])
-    s2 = [s2_flat + c["s2"][3] * face_sum[a] + c["s2"][4] * edge_square[a] for a in range(3)]
-    shear = [c["s2_mixed"][0] * mixed[e] for e in range(3)]
-    xy, xz, yz = shear
-    turned = [
-        s2[0] * vel[0] + xy * vel[1] + xz * vel[2],
-        xy * vel[0] + s2[1] * vel[1] + yz * vel[2],
-        xz * vel[0] + yz * vel[1] + s2[2] * vel[2],
+        return f[0] * count + (f[1] - f[0]) * twice
+
+    s0 = c["s0"][0] * rest + c["s0"][1] * face_total + c["s0"][2] * edge_total
+    s2_flat = by_class([9.0 * f for f in c["s2"][:3]])
+    s2 = [s2_flat + (9.0 * c["s2"][3]) * face_sum[a] + (9.0 * c["s2"][4]) * edge_square[a] for a in range(3)]
+    xy, xz, yz = [(9.0 * c["s2_mixed"][0]) * mixed[e] for e in range(3)]
+    s0_thrice = 3.0 * s0
+    bend = [
+        (s2[0] - s0_thrice) * vel[0] + xy * vel[1] + xz * vel[2],
+        xy * vel[0] + (s2[1] - s0_thrice) * vel[1] + yz * vel[2],
+        xz * vel[0] + yz * vel[1] + (s2[2] - s0_thrice) * vel[2],
     ]
-    bend = [3.0 * turned[a] - vel[a] * s0 for a in range(3)]
-    density = s0 - 1.5 * (vel[0] * bend[0] + vel[1] * bend[1] + vel[2] * bend[2])
-    open_part = 1.0 - blocking
-    momentum = []
-    for a in range(3):
-        s1 = c["s1"][0] * face_diff[a] + c["s1"][1] * edge_diff[a]
-        slope = c["odd"][0] * (face_diff[a] + edge_diff[a]) + 3.0 * (s1 + bend[a])
-        slope = open_part * slope
-        momentum.append(slope + blocking if a == 0 else slope)
+    density = s0 - 0.5 * (vel[0] * bend[0] + vel[1] * bend[1] + vel[2] * bend[2])
+    by_face, by_edge = c["odd"][0] + 3.0 * c["s1"][0], c["odd"][0] + 3.0 * c["s1"][1]
+    momentum = [open_part * (by_face * face_diff[a] + by_edge * edge_diff[a] + bend[a]) for a in range(3)]
+    momentum[0] = momentum[0] + blocking
     even = open_part * (by_class(c["even"]) + density)
-    sq_flat = by_class(c["square"][:3])
-    square = [open_part * (sq_flat + c["square"][3] * face_sum[a] + c["square"][4] * edge_square[a]) for a in range(3)]
-    cross = [(c["mixed"][0] * open_part) * mixed[e] for e in range(3)]
-    keep_sum = 0.6 * blocking - 0.1
-    keep_diff = -0.1 - 0.4 * blocking
+    flat = open_part * by_class(c["square"][:3])
+    square = [open_square * (face_sum[a] + edge_square[a]) for a in range(3)]
+    cross = [open_mixed * mixed[e] for e in range(3)]
+    at_face = even + flat
+    at_edge = at_face + flat
     out = [None] * 19
-    out[0] = (2.0 * keep_sum) * rest + even
+    out[0] = (keep_sum + keep_sum) * rest + even
     for a, (i, j) in enumerate(FACES):
-        half = keep_sum * face_sum[a] + (even + square[a])
+        half = keep_sum * face_sum[a] + (at_face + square[a])
         tilt = keep_diff * face_diff[a] + momentum[a]
         out[i], out[j] = half + tilt, half - tilt
     for e, (dims, same, cross_pair) in enumerate(EDGES):
         p, q = dims
-        level = even + square[p] + square[q]
+        level = at_edge + (square[p] + square[q])
         half = keep_sum * edge[e][0] + (level + cross[e])
         tilt = keep_diff * edge[e][1] + (momentum[p] + momentum[q])
         out[same[0]], out[same[1]] = half + tilt, half - tilt
@@ -189,6 +202,46 @@
     return 0 if sign == 1 else 1
 
 
+def read_cells(cells, face, columns, corner, extent, x, h):
+    nx, ny, nz = extent
+    lane = lax.broadcasted_iota(jnp.int32, (8, nz), 1)
+    read = []
+    for i, (dx, dy, dz) in enumerate(VELOCITY):
+        from_x = x + dx
+        outside = not 0 <= from_x < nx
+        rows = slice(BODY + 8 * h + dy, BODY + 8 * h + dy + 8)
+        if outside:
+            value = face[slot(dx), ALONG[0][dx].index(i), rows, :]
+        else:
+            value = cells[i, from_x, rows, :]
+        if dz:
+            last = nz - 1 if dz == 1 else 0
+            if outside:
+                column = corner[slot(dx) * 2 + slot(dz)]
+                turn = (last - h) % nz
+            else:
+                column = columns[slot(dz), rows, :]
+                turn = (last - ALONG[2][dz].index(i) * nx - from_x) % nz
+            column = pltpu.roll(column, turn, 1) if turn else column
+            value = jnp.where(lane == last, column, pltpu.roll(value, nz - 1 if dz == 1 else 1, 1))
+        read.append(value)
+    return read
+
+
+def one_level(cells, face, columns, corner, terms, factors, extent, x, h):
+    rows = slice(8 * h, 8 * h + 8)
+    read = read_cells(cells, face, columns, corner, extent, x, h)
+    vel = [terms[a, x, rows, :] for a in range(3)]
+    return pull_back(read, vel, [factors[j, x, rows, :] for j in range(FACTORS)])
+
+
+def weigh(terms, weighed, x, rows):
+    total = weighed[0] * terms[3, x, rows, :]
+    for j in range(1, 19):
+        total = total + weighed[j] * terms[3 + j, x, rows, :]
+    return total
+
+
 def member_at(velocity):
     return VELOCITY.index(velocity)
 
@@ -203,25 +256,33 @@
     adjoint,
     porosity,
     solid,
-    out_adjoint,
+    out_inner,
     out_grad,
     out_drag,
+    level_one,
+    marks,
+    factors,
+    terms_last,
+    face_last,
+    columns_last,
+    corner_last,
     level_two,
-    level_one,
     states,
     porous,
-    marks,
-    block,
-    terms,
+    terms_first,
     sums,
     face_send,
     rows_send,
     columns_send,
-    face_recv,
+    xy_send,
+    xz_send,
+    yz_send,
+    face_first,
     rows_recv,
-    columns_recv,
-    rows_edge,
-    columns_edge,
+    columns_first,
+    xy_recv,
+    corner_first,
+    yz_recv,
     drag_row,
     drag_slots,
     meter,
@@ -233,6 +294,10 @@
     sx, sy, sz = mesh_sizes
     nx, ny, nz = extent
     halves = ny // 8
+    terms = (terms_first, terms_last)
+    face_recv = (face_first, face_last)
+    columns_recv = (columns_first, columns_last)
+    xz_recv = (corner_first, corner_last)
     body = pl.ds(BODY, ny)
     inner = tuple(range(1, nx - 1))
     outer = (0, nx - 1)
@@ -281,9 +346,14 @@
         return (lax.rem(pair + h, pairs) * 2 + core, lax.rem(me[1] + y, sy), me[2])
 
     barrier = pltpu.get_barrier_semaphore()
-    targets = [first_partner(c, z) for c, z in first_group if (c, z) not in ((0, 1), (0, sz - 1))]
-    targets += [second_partner(h, y) for h, y in second_group if (h, y) not in ((0, 1), (0, sy - 1))]
-    targets += [shifted(offset) for offset in around]
+    far = [(z, 1, first_partner(c, z)) for c, z in first_group if (c, z) not in ((0, 1), (0, sz - 1))]
+    far = [(min(z, sz - z), n, target) for z, n, target in far]
+    for h, y in second_group:
+        if (h, y) not in ((0, 1), (0, sy - 1)):
+            far.append((2 * h + (min(y, sy - y) + 1) // 2, 2, second_partner(h, y)))
+    for offset in around:
+        far.append((2 * abs(offset[0]) + abs(offset[1]) + abs(offset[2]), 3, shifted(offset)))
+    targets = [entry[2] for entry in sorted(far, key=lambda entry: -entry[0])]
     for target in targets:
         pl.semaphore_signal(barrier, inc=1, device_id=target, device_id_type=MESH)
 
@@ -313,33 +383,44 @@
                 for x in planes:
                     rows_send[step, at, k * nx + x : k * nx + x + 1, :] = cells[i, x, edge_row : edge_row + 1, :]
 
+    def pack_edges(step, cells):
+        for p in (1, -1):
+            near = 0 if p == 1 else nx - 1
+            for q in (1, -1):
+                i = member_at((p, q, 0))
+                row = BODY if q == 1 else BODY + ny - 1
+                xy_send[step, slot(p) * 2 + slot(q)] = cells[i, near, row : row + 1, :]
+                i = member_at((p, 0, q))
+                packed = None
+                for h in range(halves):
+                    column = cells[i, near, BODY + 8 * h : BODY + 8 * h + 8, :]
+                    turn = (h if q == 1 else h + 1) % nz
+                    column = pltpu.roll(column, turn, 1) if turn else column
+                    packed = column if packed is None else jnp.where(lane == h, column, packed)
+                xz_send[step, slot(p) * 2 + slot(q)] = packed
+                row = 0 if p == 1 else ny - 1
+                yz_send[step, slot(p) * 2 + slot(q)] = columns_send[step, slot(q), row : row + 1, :]
+
     def message(step, direction):
         dx, dy, dz = direction
         if dx and not dy and not dz:
             source = face_send.at[step, slot(dx)]
-            target = face_recv.at[step, slot(dx), :, body, :]
-            tiles = 5 * halves
+            target = face_recv[step].at[slot(dx), :, body, :]
         elif dy and not dx and not dz:
             source = rows_send.at[step, slot(dy)]
             target = rows_recv.at[step, slot(dy)]
-            tiles = rows_send.shape[2] // 8
         elif dz and not dx and not dy:
             source = columns_send.at[step, slot(dz)]
-            target = columns_recv.at[step, slot(dz), body, :]
-            tiles = halves
+            target = columns_recv[step].at[slot(dz), body, :]
         elif not dz:
-            source = rows_send.at[step, slot(dy), pl.ds(xy_row(dx, dy) // 8 * 8, 8), :]
-            target = rows_edge.at[step, slot(dx) * 2 + slot(dy)]
-            tiles = 1
+            source = xy_send.at[step, slot(dx) * 2 + slot(dy)]
+            target = xy_recv.at[step, slot(dx) * 2 + slot(dy)]
         elif not dy:
-            source = columns_send.at[step, slot(dz)]
-            target = columns_edge.at[step, slot(dx) * 2 + slot(dz)]
-            tiles = halves
+            source = xz_send.at[step, slot(dx) * 2 + slot(dz)]
+            target = xz_recv[step].at[slot(dx) * 2 + slot(dz)]
         else:
-            near, far = (0, BODY + ny) if dy == 1 else (ny - 8, BODY - 8)
-            source = columns_send.at[step, slot(dz), pl.ds(near, 8), :]
-            target = columns_recv.at[step, slot(dz), pl.ds(far, 8), :]
-            tiles = 1
+            source = yz_send.at[step, slot(dy) * 2 + slot(dz)]
+            target = yz_recv.at[step, slot(dy) * 2 + slot(dz)]
         copy = pltpu.make_async_remote_copy(
             src_ref=source,
             dst_ref=target,
@@ -348,23 +429,15 @@
             device_id=shifted(tuple(-d for d in direction)),
             device_id_type=MESH,
         )
-        return copy, tiles
+        return copy
 
     def send(step, directions):
-        total = 0
         for direction in directions:
-            copy, tiles = message(step, direction)
-            copy.start()
-            total += tiles
-        return total
-
-    def await_tiles(tiles, semaphore):
-        whole = meter.at[pl.ds(0, tiles)]
+            message(step, direction).start()
+
+    def await_rows(rows, semaphore):
+        whole = meter.at[pl.ds(0, rows)]
         pltpu.make_async_copy(whole, whole, semaphore).wait()
-
-    def xy_row(dx, dy):
-        k = ALONG[1][dy].index(member_at((dx, dy, 0)))
-        return k * nx + (0 if dx == 1 else nx - 1)
 
     def halo_row(sign):
         return BODY + ny if sign == 1 else BODY - 1
@@ -377,52 +450,22 @@
                     if 0 <= x - VELOCITY[i][0] < nx:
                         got = rows_recv[step, slot(sign), k * nx + x : k * nx + x + 1, :]
                         cells[i, x, row : row + 1, :] = got
+            for t in (1, -1):
+                columns_recv[step][slot(t), row : row + 1, :] = yz_recv[step, slot(sign) * 2 + slot(t)]
 
     def insert_edges(step):
         for dx in (1, -1):
             for dy in (1, -1):
                 k = ALONG[0][dx].index(member_at((dx, dy, 0)))
-                r = xy_row(dx, dy) % 8
                 row = halo_row(dy)
-                face_recv[step, slot(dx), k, row : row + 1, :] = rows_edge[step, slot(dx) * 2 + slot(dy), r : r + 1, :]
-
-    def read_cells(step, cells, x, h):
-        read = []
-        for i, (dx, dy, dz) in enumerate(VELOCITY):
-            from_x = x + dx
-            outside = not 0 <= from_x < nx
-            rows = slice(BODY + 8 * h + dy, BODY + 8 * h + dy + 8)
-            if outside:
-                value = face_recv[step, slot(dx), ALONG[0][dx].index(i), rows, :]
-            else:
-                value = cells[i, from_x, rows, :]
-            if dz:
-                spot = ALONG[2][dz].index(i) * nx + from_x % nx
-                if outside:
-                    column = columns_edge[step, slot(dx) * 2 + slot(dz), 8 * h : 8 * h + 8, :]
-                else:
-                    column = columns_recv[step, slot(dz), rows, :]
-                last = nz - 1 if dz == 1 else 0
-                turn = (last - spot) % nz
-                column = pltpu.roll(column, turn, 1) if turn else column
-                value = jnp.where(lane == last, column, pltpu.roll(value, nz - 1 if dz == 1 else 1, 1))
-            read.append(value)
-        return read
+                face_recv[step][slot(dx), k, row : row + 1, :] = xy_recv[step, slot(dx) * 2 + slot(dy)]
 
     def level(step, cells, x, h):
-        rows = slice(8 * h, 8 * h + 8)
-        read = read_cells(step, cells, x, h)
-        vel = [terms[step, a, x, rows, :] for a in range(3)]
-        return pull_back(read, vel, block[x, rows, :])
-
-    def gradient(step, weighed, x, rows):
-        total = weighed[0] * terms[step, 3, x, rows, :]
-        for j in range(1, 19):
-            total = total + weighed[j] * terms[step, 3 + j, x, rows, :]
-        return total
+        return one_level(cells, face_recv[step], columns_recv[step], xz_recv[step], terms[step], factors, extent, x, h)
 
     loads[0].wait()
     pack(0, level_two, range(nx), False)
+    pack_edges(0, level_two)
     for load in loads[1:]:
         load.wait()
     total = jnp.zeros((8, nz), F32)
@@ -430,7 +473,8 @@
         for h in range(halves):
             rows = slice(8 * h, 8 * h + 8)
             closed = jnp.where(marks[x, rows, :] == 0, porous[x, rows, :], 1.0)
-            block[x, rows, :] = closed
+            for j, value in enumerate(blocking_factors(closed)):
+                factors[j, x, rows, :] = value
             flux = None
             for t in range(2):
                 gain = sum(states[t, i, x, rows, :] for i in ALONG[0][1])
@@ -444,9 +488,9 @@
 
     pl.semaphore_wait(barrier, len(targets))
 
-    sent = send(0, around)
-    near_tiles = sum(message_tiles(d, nx, halves) for d in near_part)
-    side_tiles = sum(message_tiles(d, nx, halves) for d in side_part)
+    send(0, around)
+    near_rows = sum(message_rows(d, extent) for d in near_part)
+    side_rows = sum(message_rows(d, extent) for d in side_part)
 
     mine_first = core * sz + me[2]
     mine_second = pair * sy + me[1]
@@ -465,10 +509,6 @@
                 device_id_type=MESH,
             ).start()
 
-    def await_rows(target, count, semaphore):
-        whole = target.at[pl.ds(0, count)]
-        pltpu.make_async_copy(whole, whole, semaphore).wait()
-
     drag_send(0, drag_first, mine_first, first_group, first_partner)
 
     for step, t in ((0, 1), (1, 0)):
@@ -477,7 +517,7 @@
                 rows = slice(8 * h, 8 * h + 8)
                 vel, _, weights = primal_terms([states[t, i, x, rows, :] for i in range(19)])
                 for j, value in enumerate(vel + weights):
-                    terms[step, j, x, rows, :] = value
+                    terms[step][j, x, rows, :] = value
 
     def first_level(x):
         for h in range(halves):
@@ -491,19 +531,20 @@
                     for k, i in enumerate(ALONG[0][sign]):
                         face_send[1, slot(sign), k, rows, :] = fresh[i]
 
-    await_tiles(near_tiles, recv_sem.at[0, 0])
+    await_rows(near_rows, recv_sem.at[0, 0])
     insert_rows(0, level_two)
     for x in inner:
         first_level(x)
     pack(1, level_one, inner, False)
-    await_tiles(side_tiles, recv_sem.at[0, 1])
+    await_rows(side_rows, recv_sem.at[0, 1])
     insert_edges(0)
     for x in outer:
         first_level(x)
     pack(1, level_one, outer, True)
-    sent += send(1, around)
-
-    await_rows(drag_first, len(first_group), drag_sem.at[0])
+    pack_edges(1, level_one)
+    send(1, around)
+
+    await_rows(len(first_group), drag_sem.at[0])
     drag_row[1] = jnp.sum(drag_first[...], axis=0)
     drag_send(1, drag_second, mine_second, second_group, second_partner)
 
@@ -511,52 +552,81 @@
         for h in range(halves):
             rows = slice(8 * h, 8 * h + 8)
             weighed = [sums[j, x, rows, :] for j in range(19)]
-            out_grad[x, rows, :] = out_grad[x, rows, :] + gradient(0, weighed, x, rows)
+            out_grad[x, rows, :] = out_grad[x, rows, :] + weigh(terms[0], weighed, x, rows)
 
     def second_level(x):
         for h in range(halves):
             rows = slice(8 * h, 8 * h + 8)
             fresh, weighed = level(1, level_one, x, h)
             for i in range(19):
-                out_adjoint[i, x, rows, :] = fresh[i]
-            total = out_grad[x, rows, :] + gradient(1, weighed, x, rows)
+                out_inner[i, x - 1, rows, :] = fresh[i]
+            total = out_grad[x, rows, :] + weigh(terms[1], weighed, x, rows)
             out_grad[x, rows, :] = jnp.where(marks[x, rows, :] == 0, total, 0.0)
 
-    await_tiles(near_tiles, recv_sem.at[1, 0])
+    await_rows(near_rows, recv_sem.at[1, 0])
     insert_rows(1, level_one)
     for x in inner:
         second_level(x)
-    await_tiles(side_tiles, recv_sem.at[1, 1])
+    await_rows(side_rows, recv_sem.at[1, 1])
     insert_edges(1)
-    for x in outer:
-        second_level(x)
-
-    await_rows(drag_second, len(second_group), drag_sem.at[1])
+
+    await_rows(len(second_group), drag_sem.at[1])
     everyone = jnp.sum(drag_second[...], axis=0)
     cells_in_all = nx * ny * nz * sx * sy * sz
-    out_drag[...] = jnp.broadcast_to(everyone * (1.0 / cells_in_all), (8, nz))
-
-    await_tiles(sent, send_sem.at[0])
-    await_rows(drag_slots, len(first_group) + len(second_group), drag_sem.at[2])
-
-
-def message_tiles(direction, nx, halves):
+    out_drag[...] = jnp.broadcast_to(jnp.sum(everyone, axis=1, keepdims=True) * (1.0 / cells_in_all), (8, nz))
+
+    await_rows(2 * (near_rows + side_rows), send_sem.at[0])
+    await_rows(len(first_group) + len(second_group), drag_sem.at[2])
+
+
+def message_rows(direction, extent):
+    nx, ny, nz = extent
     dx, dy, dz = (d != 0 for d in direction)
-    if dx and not dy and not dz:
-        return 5 * halves
-    if dy and not dx and not dz:
-        return -(-5 * nx // 8)
-    return halves if dz and not dy else 1
-
-
-def put_out(adjoint, gradient, drag, out_adjoint, out_gradient, out_drag, sem):
-    copies = [
-        pltpu.make_async_copy(adjoint, out_adjoint, sem.at[0]),
-        pltpu.make_async_copy(gradient, out_gradient, sem.at[1]),
-    ]
-    for copy in copies:
-        copy.start()
-    out_drag[...] = jnp.sum(drag[0:1, :], axis=1, keepdims=True)
+    if dx + dy + dz == 1:
+        return 5 * ny if dx else -(-5 * nx // 8) * 8 if dy else ny
+    return 8 if dx and dz else 1
+
+
+def finish(
+    extent,
+    inner,
+    grad,
+    drag,
+    cells,
+    marks,
+    factors,
+    terms,
+    face,
+    columns,
+    corner,
+    out_adjoint,
+    out_grad,
+    out_drag,
+    outer,
+    grad_whole,
+    total,
+    sem,
+):
+    nx, ny, nz = extent
+    copies = [pltpu.make_async_copy(inner, out_adjoint.at[:, pl.ds(1, nx - 2)], sem.at[0])]
+    copies[0].start()
+    total[...] = drag[0:1, 0:1]
+    copies.append(pltpu.make_async_copy(total, out_drag, sem.at[1]))
+    copies[1].start()
+    for n, x in enumerate((0, nx - 1)):
+        for h in range(ny // 8):
+            rows = slice(8 * h, 8 * h + 8)
+            fresh, weighed = one_level(cells, face, columns, corner, terms, factors, extent, x, h)
+            for i in range(19):
+                outer[n, i, rows, :] = fresh[i]
+            slope = grad[x, rows, :] + weigh(terms, weighed, x, rows)
+            grad_whole[x, rows, :] = jnp.where(marks[x, rows, :] == 0, slope, 0.0)
+        copies.append(pltpu.make_async_copy(outer.at[n], out_adjoint.at[:, x], sem.at[2 + n]))
+        copies[-1].start()
+    for x in range(1, nx - 1):
+        grad_whole[x] = grad[x]
+    copies.append(pltpu.make_async_copy(grad_whole, out_grad, sem.at[4]))
+    copies[-1].start()
     for copy in copies:
         copy.wait()
 
@@ -578,32 +648,40 @@
             functools.partial(kernel, sizes, (nx, ny, nz)),
             name="adjoint_window",
             out_shape=(
-                pltpu.VMEM((19, nx, ny, nz), F32),
+                pltpu.VMEM((19, nx - 2, ny, nz), F32),
                 pltpu.VMEM((nx, ny, nz), F32),
                 pltpu.VMEM((8, nz), F32),
+                pltpu.VMEM((19, nx, padded, nz), F32),
+                pltpu.VMEM((nx, ny, nz), jnp.int32),
+                pltpu.VMEM((FACTORS, nx, ny, nz), F32),
+                pltpu.VMEM((22, nx, ny, nz), F32),
+                pltpu.VMEM((2, 5, padded, nz), F32),
+                pltpu.VMEM((2, padded, nz), F32),
+                pltpu.VMEM((4, 8, nz), F32),
             ),
             in_specs=[hbm] * 4,
-            out_specs=(vmem, vmem, vmem),
+            out_specs=(vmem,) * 10,
             scratch_shapes=[
-                pltpu.VMEM((19, nx, padded, nz), F32),
                 pltpu.VMEM((19, nx, padded, nz), F32),
                 pltpu.VMEM((2, 19, nx, ny, nz), F32),
                 pltpu.VMEM((nx, ny, nz), F32),
-                pltpu.VMEM((nx, ny, nz), jnp.int32),
-                pltpu.VMEM((nx, ny, nz), F32),
-                pltpu.VMEM((2, 22, nx, ny, nz), F32),
+                pltpu.VMEM((22, nx, ny, nz), F32),
                 pltpu.VMEM((19, nx, ny, nz), F32),
                 pltpu.VMEM((2, 2, 5, ny, nz), F32),
                 pltpu.VMEM((2, 2, row_tiles, nz), F32),
                 pltpu.VMEM((2, 2, ny, nz), F32),
-                pltpu.VMEM((2, 2, 5, padded, nz), F32),
+                pltpu.VMEM((2, 4, 1, nz), F32),
+                pltpu.VMEM((2, 4, 8, nz), F32),
+                pltpu.VMEM((2, 4, 1, nz), F32),
+                pltpu.VMEM((2, 5, padded, nz), F32),
                 pltpu.VMEM((2, 2, row_tiles, nz), F32),
-                pltpu.VMEM((2, 2, padded, nz), F32),
-                pltpu.VMEM((2, 4, 8, nz), F32),
-                pltpu.VMEM((2, 4, ny, nz), F32),
+                pltpu.VMEM((2, padded, nz), F32),
+                pltpu.VMEM((2, 4, 1, nz), F32),
+                pltpu.VMEM((4, 8, nz), F32),
+                pltpu.VMEM((2, 4, 1, nz), F32),
                 pltpu.VMEM((2, 1, nz), F32),
                 pltpu.VMEM((2 * sizes[2] + sizes[0] // 2 * sizes[1], 1, nz), F32),
-                pltpu.VMEM((128, 8, nz), F32),
+                pltpu.VMEM((1024, 1, nz), F32),
                 pltpu.SemaphoreType.DMA((5,)),
                 pltpu.SemaphoreType.DMA((1,)),
                 pltpu.SemaphoreType.DMA((2, 2)),
@@ -614,17 +692,22 @@
             ),
         )(*arguments)
         adjoint, gradient, drag = pl.pallas_call(
-            put_out,
-            name="put_out",
+            functools.partial(finish, (nx, ny, nz)),
+            name="finish",
             out_shape=(
                 jax.ShapeDtypeStruct((19, nx, ny, nz), F32),
                 jax.ShapeDtypeStruct((nx, ny, nz), F32),
                 jax.ShapeDtypeStruct((1, 1), F32),
             ),
-            in_specs=[vmem] * 3,
-            out_specs=(hbm, hbm, vmem),
-            scratch_shapes=[pltpu.SemaphoreType.DMA((2,))],
-            compiler_params=pltpu.CompilerParams(vmem_limit_bytes=1 << 20),
+            in_specs=[vmem] * 10,
+            out_specs=(hbm, hbm, hbm),
+            scratch_shapes=[
+                pltpu.VMEM((2, 19, ny, nz), F32),
+                pltpu.VMEM((nx, ny, nz), F32),
+                pltpu.VMEM((1, 1), F32),
+                pltpu.SemaphoreType.DMA((5,)),
+            ],
+            compiler_params=pltpu.CompilerParams(vmem_limit_bytes=2 << 20),
         )(*results)
         return adjoint, gradient, drag.reshape(())
 

time: 24.2 us -> 23.1 us (0.955)
  Pallas kernels: 23.4 us -> 22.4 us
    pallas_call x1, Pallas kernels: 22 us -> 21.4 us  [body(): pl.pallas_call(functools.partial(kernel, sizes, (nx, ny, nz)), name='adjo...]
    pallas_call x1, Pallas kernels: 1.36 us -> 0.99 us  [body(): pl.pallas_call(functools.partial(finish, (nx, ny, nz)), name='finish', ou...]
where the time goes in v2:
time: 23.1 us; the launch traced here: 23 us
  Pallas kernels  22.4 us (97%)
  between operations  0.64 us (3%)
    pallas_call x1, Pallas kernels, body(): pl.pallas_call(functools.partial(kernel, sizes, (nx, ny, nz)), name='adjo...  21.4 us
    pallas_call x1, Pallas kernels, body(): pl.pallas_call(functools.partial(finish, (nx, ny, nz)), name='finish', ou...  0.99 us

profile of v2, /device:TPU:1, one launch (start us, length us, event | category | flops | bytes accessed | tf_op | source)
XLA Modules:
  0.0 23.0 jit_solution(16391875085783622171)
XLA Ops:
  0.6 21.4 %adjoint_window.1 = (f32[19,2,16,128]{3,2,1,0:T(8,128)S(1)}, f32[4,16,128]{2,1,0:T(8,128)S(1)}, f32[8,128]{1,0:T(8,128)S(1)}, f32[19,4,32,128]{3,2,1,0:T(8,128)S...) custom-call(f32[2,19,4,16,128]{4,3,2,1,0:T(8,128)} %primal.1, ...), custom_call_target="tpu_custom_call" | custom-call | tf_op jit(solution)/shard_map/adjoint_window/pallas_call | solution.py:647
  22.0 1.0 %finish.1 = (f32[19,4,16,128]{3,2,1,0:T(8,128)}, f32[4,16,128]{2,1,0:T(8,128)}, f32[1,1]{1,0:T(1,128)}) custom-call(f32[19,2,16,128]{3,2,1,0:T(8,128)S(1)} %get-tuple-element.16.inner, f32[4,16,128]{2,1,0:T(8,128)S(1)} %get-tuple-element.17.grad, f32[8,128]{1,0:T(8,128)S(1)} %get-tuple-element.18.drag, f32[19,4,32,128]{3,2,1,0:T(8,128)S(1)} %get-tuple-element.19.cells, ...), custom_call_target="tpu_custom_call" | custom-call | tf_op jit(solution)/shard_map/finish/pallas_call | solution.py:694

commit v3 on v2

--- a/solution.py
+++ b/solution.py
@@ -132,6 +132,27 @@
     return vel, flux[0], [rest] + even + odd
 
 
+class Nothing:
+    def __add__(self, other):
+        return other
+
+    __radd__ = __add__
+
+    def __sub__(self, other):
+        return -other
+
+    def __rsub__(self, other):
+        return other
+
+    def __mul__(self, other):
+        return self
+
+    __rmul__ = __mul__
+
+    def __neg__(self):
+        return self
+
+
 FACTORS = 6
 
 
@@ -147,7 +168,7 @@
     ]
 
 
-def pull_back(read, vel, factors):
+def pull_back(read, vel, factors, source=True):
     c = COEF
     blocking, open_part, open_square, open_mixed, keep_sum, keep_diff = factors
     face_sum, face_diff, edge, mixed, edge_square, edge_diff, face_total, edge_total = pair_sums(read)
@@ -171,7 +192,8 @@
     density = s0 - 0.5 * (vel[0] * bend[0] + vel[1] * bend[1] + vel[2] * bend[2])
     by_face, by_edge = c["odd"][0] + 3.0 * c["s1"][0], c["odd"][0] + 3.0 * c["s1"][1]
     momentum = [open_part * (by_face * face_diff[a] + by_edge * edge_diff[a] + bend[a]) for a in range(3)]
-    momentum[0] = momentum[0] + blocking
+    if source:
+        momentum[0] = momentum[0] + blocking
     even = open_part * (by_class(c["even"]) + density)
     flat = open_part * by_class(c["square"][:3])
     square = [open_square * (face_sum[a] + edge_square[a]) for a in range(3)]
@@ -233,6 +255,56 @@
     read = read_cells(cells, face, columns, corner, extent, x, h)
     vel = [terms[a, x, rows, :] for a in range(3)]
     return pull_back(read, vel, [factors[j, x, rows, :] for j in range(FACTORS)])
+
+
+def corner_members(dy):
+    return ((member_at((0, dy, dy)), dy), (member_at((0, dy, -dy)), -dy))
+
+
+def corner_tile(extent, dy):
+    return (extent[1] // 8 - 1, 7) if dy == 1 else (0, 0)
+
+
+def corner_change(got, extent, dy, x):
+    nx, ny, nz = extent
+    lane = lax.broadcasted_iota(jnp.int32, (8, nz), 1)
+    row = lax.broadcasted_iota(jnp.int32, (8, nz), 0)
+    change = jnp.zeros((8, nz), F32)
+    for i, dz in corner_members(dy):
+        last = nz - 1 if dz == 1 else 0
+        turn = (last - ALONG[2][dz].index(i) * nx - x) % nz
+        value = jnp.broadcast_to(got[slot(dy) * 2 + slot(dz)], (8, nz))
+        value = pltpu.roll(value, turn, 1) if turn else value
+        change = jnp.where(lane == last, value, change)
+    return jnp.where(row == corner_tile(extent, dy)[1], change, 0.0)
+
+
+def corner_response(terms, factors, extent, dy, x):
+    nx, ny, nz = extent
+    h, at = corner_tile(extent, dy)
+    rows = slice(8 * h, 8 * h + 8)
+    lane = lax.broadcasted_iota(jnp.int32, (8, nz), 1)
+    row = lax.broadcasted_iota(jnp.int32, (8, nz), 0)
+    read = [Nothing()] * 19
+    for i, dz in corner_members(dy):
+        read[i] = jnp.where((row == at) & (lane == (nz - 1 if dz == 1 else 0)), 1.0, 0.0)
+    vel = [terms[a, x, rows, :] for a in range(3)]
+    return pull_back(read, vel, [factors[j, x, rows, :] for j in range(FACTORS)], source=False)[0]
+
+
+def corner_weight(terms, extent, dy, x):
+    nx, ny, nz = extent
+    h = corner_tile(extent, dy)[0]
+    rows = slice(8 * h, 8 * h + 8)
+    lane = lax.broadcasted_iota(jnp.int32, (8, nz), 1)
+    even, odd = 3 + 1 + 3 + 4, 3 + 1 + 9 + 3 + 4
+    same, cross = [
+        terms[even + n, x, rows, :] + terms[odd + n, x, rows, :]
+        if dy == 1
+        else terms[even + n, x, rows, :] - terms[odd + n, x, rows, :]
+        for n in range(2)
+    ]
+    return jnp.where(lane == (nz - 1 if dy == 1 else 0), same, cross)
 
 
 def weigh(terms, weighed, x, rows):
@@ -283,6 +355,7 @@
     xy_recv,
     corner_first,
     yz_recv,
+    response,
     drag_row,
     drag_slots,
     meter,
@@ -331,7 +404,8 @@
         for t in (1, -1)
     ]
     around = edges + faces
-    near_part = [d for d in around if not d[0]]
+    corner_part = [d for d in edges if not d[0]]
+    near_part = [d for d in faces if not d[0]]
     side_part = [d for d in around if d[0]]
 
     pair, core = me[0] // 2, me[0] % 2
@@ -425,7 +499,7 @@
             src_ref=source,
             dst_ref=target,
             send_sem=send_sem.at[0],
-            recv_sem=recv_sem.at[step, 1 if dx else 0],
+            recv_sem=recv_sem.at[step, 1 if dx else 2 if dy and dz else 0],
             device_id=shifted(tuple(-d for d in direction)),
             device_id_type=MESH,
         )
@@ -450,8 +524,6 @@
                     if 0 <= x - VELOCITY[i][0] < nx:
                         got = rows_recv[step, slot(sign), k * nx + x : k * nx + x + 1, :]
                         cells[i, x, row : row + 1, :] = got
-            for t in (1, -1):
-                columns_recv[step][slot(t), row : row + 1, :] = yz_recv[step, slot(sign) * 2 + slot(t)]
 
     def insert_edges(step):
         for dx in (1, -1):
@@ -463,6 +535,11 @@
     def level(step, cells, x, h):
         return one_level(cells, face_recv[step], columns_recv[step], xz_recv[step], terms[step], factors, extent, x, h)
 
+    nothing = jnp.zeros((1, nz), F32)
+    for columns in columns_recv:
+        for at in range(2):
+            columns[at, BODY - 1 : BODY, :] = nothing
+            columns[at, BODY + ny : BODY + ny + 1, :] = nothing
     loads[0].wait()
     pack(0, level_two, range(nx), False)
     pack_edges(0, level_two)
@@ -491,6 +568,7 @@
     send(0, around)
     near_rows = sum(message_rows(d, extent) for d in near_part)
     side_rows = sum(message_rows(d, extent) for d in side_part)
+    corner_rows = sum(message_rows(d, extent) for d in corner_part)
 
     mine_first = core * sz + me[2]
     mine_second = pair * sy + me[1]
@@ -519,6 +597,12 @@
                 for j, value in enumerate(vel + weights):
                     terms[step][j, x, rows, :] = value
 
+    for step in range(2):
+        for x in range(nx) if step == 0 else inner:
+            for dy in (1, -1):
+                for i, value in enumerate(corner_response(terms[step], factors, extent, dy, x)):
+                    response[step, slot(dy), i, x] = value
+
     def first_level(x):
         for h in range(halves):
             fresh, weighed = level(0, level_two, x, h)
@@ -526,21 +610,30 @@
             for i in range(19):
                 level_one[i, x, BODY + 8 * h : BODY + 8 * h + 8, :] = fresh[i]
                 sums[i, x, rows, :] = weighed[i]
-            for sign, near in ((1, 0), (-1, nx - 1)):
-                if x == near:
-                    for k, i in enumerate(ALONG[0][sign]):
-                        face_send[1, slot(sign), k, rows, :] = fresh[i]
+
+    def first_corners(x):
+        for dy in (1, -1):
+            h = corner_tile(extent, dy)[0]
+            change = corner_change(yz_recv[0], extent, dy, x)
+            for i in range(19):
+                rows = slice(BODY + 8 * h, BODY + 8 * h + 8)
+                level_one[i, x, rows, :] = level_one[i, x, rows, :] + change * response[0, slot(dy), i, x]
 
     await_rows(near_rows, recv_sem.at[0, 0])
     insert_rows(0, level_two)
     for x in inner:
         first_level(x)
-    pack(1, level_one, inner, False)
     await_rows(side_rows, recv_sem.at[0, 1])
     insert_edges(0)
     for x in outer:
         first_level(x)
-    pack(1, level_one, outer, True)
+    await_rows(corner_rows, recv_sem.at[0, 2])
+    for x in outer + inner:
+        first_corners(x)
+    for sign, near in ((1, 0), (-1, nx - 1)):
+        for k, i in enumerate(ALONG[0][sign]):
+            face_send[1, slot(sign), k] = level_one[i, near, body, :]
+    pack(1, level_one, range(nx), False)
     pack_edges(1, level_one)
     send(1, around)
 
@@ -552,7 +645,12 @@
         for h in range(halves):
             rows = slice(8 * h, 8 * h + 8)
             weighed = [sums[j, x, rows, :] for j in range(19)]
-            out_grad[x, rows, :] = out_grad[x, rows, :] + weigh(terms[0], weighed, x, rows)
+            total = out_grad[x, rows, :] + weigh(terms[0], weighed, x, rows)
+            for dy in (1, -1):
+                if h == corner_tile(extent, dy)[0]:
+                    change = corner_change(yz_recv[0], extent, dy, x)
+                    total = total + change * corner_weight(terms[0], extent, dy, x)
+            out_grad[x, rows, :] = total
 
     def second_level(x):
         for h in range(halves):
@@ -569,13 +667,27 @@
         second_level(x)
     await_rows(side_rows, recv_sem.at[1, 1])
     insert_edges(1)
+    await_rows(corner_rows, recv_sem.at[1, 2])
+    for x in inner:
+        for dy in (1, -1):
+            h = corner_tile(extent, dy)[0]
+            rows = slice(8 * h, 8 * h + 8)
+            change = corner_change(yz_recv[1], extent, dy, x)
+            for i in range(19):
+                out_inner[i, x - 1, rows, :] = out_inner[i, x - 1, rows, :] + change * response[1, slot(dy), i, x]
+            slope = change * corner_weight(terms[1], extent, dy, x)
+            out_grad[x, rows, :] = out_grad[x, rows, :] + jnp.where(marks[x, rows, :] == 0, slope, 0.0)
+    for sign in (1, -1):
+        row = halo_row(sign)
+        for t in (1, -1):
+            columns_recv[1][slot(t), row : row + 1, :] = yz_recv[1, slot(sign) * 2 + slot(t)]
 
     await_rows(len(second_group), drag_sem.at[1])
     everyone = jnp.sum(drag_second[...], axis=0)
     cells_in_all = nx * ny * nz * sx * sy * sz
     out_drag[...] = jnp.broadcast_to(jnp.sum(everyone, axis=1, keepdims=True) * (1.0 / cells_in_all), (8, nz))
 
-    await_rows(2 * (near_rows + side_rows), send_sem.at[0])
+    await_rows(2 * (near_rows + side_rows + corner_rows), send_sem.at[0])
     await_rows(len(first_group) + len(second_group), drag_sem.at[2])
 
 
@@ -679,12 +791,13 @@
                 pltpu.VMEM((2, 4, 1, nz), F32),
                 pltpu.VMEM((4, 8, nz), F32),
                 pltpu.VMEM((2, 4, 1, nz), F32),
+                pltpu.VMEM((2, 2, 19, nx, 8, nz), F32),
                 pltpu.VMEM((2, 1, nz), F32),
                 pltpu.VMEM((2 * sizes[2] + sizes[0] // 2 * sizes[1], 1, nz), F32),
                 pltpu.VMEM((1024, 1, nz), F32),
                 pltpu.SemaphoreType.DMA((5,)),
                 pltpu.SemaphoreType.DMA((1,)),
-                pltpu.SemaphoreType.DMA((2, 2)),
+                pltpu.SemaphoreType.DMA((2, 3)),
                 pltpu.SemaphoreType.DMA((3,)),
             ],
             compiler_params=pltpu.CompilerParams(

time: 23.1 us -> 22.8 us (0.987)
  Pallas kernels: 22.4 us -> 22 us
    pallas_call x1, Pallas kernels: 21.4 us -> 21 us  [body(): pl.pallas_call(functools.partial(kernel, sizes, (nx, ny, nz)), name='adjo...]
where the time goes in v3:
time: 22.8 us; the launch traced here: 22.6 us
  Pallas kernels  22 us (96%)
  between operations  0.64 us (3%)
    pallas_call x1, Pallas kernels, body(): pl.pallas_call(functools.partial(kernel, sizes, (nx, ny, nz)), name='adjo...  21 us
    pallas_call x1, Pallas kernels, body(): pl.pallas_call(functools.partial(finish, (nx, ny, nz)), name='finish', ou...  0.99 us

profile of v3, /device:TPU:1, one launch (start us, length us, event | category | flops | bytes accessed | tf_op | source)
XLA Modules:
  0.0 22.6 jit_solution(4475558427294427774)
XLA Ops:
  0.6 21.0 %adjoint_window.1 = (f32[19,2,16,128]{3,2,1,0:T(8,128)S(1)}, f32[4,16,128]{2,1,0:T(8,128)S(1)}, f32[8,128]{1,0:T(8,128)S(1)}, f32[19,4,32,128]{3,2,1,0:T(8,128)S...) custom-call(f32[2,19,4,16,128]{4,3,2,1,0:T(8,128)} %primal.1, ...), custom_call_target="tpu_custom_call" | custom-call | tf_op jit(solution)/shard_map/adjoint_window/pallas_call | solution.py:759
  21.7 1.0 %finish.1 = (f32[19,4,16,128]{3,2,1,0:T(8,128)}, f32[4,16,128]{2,1,0:T(8,128)}, f32[1,1]{1,0:T(1,128)}) custom-call(f32[19,2,16,128]{3,2,1,0:T(8,128)S(1)} %get-tuple-element.16.inner, f32[4,16,128]{2,1,0:T(8,128)S(1)} %get-tuple-element.17.grad, f32[8,128]{1,0:T(8,128)S(1)} %get-tuple-element.18.drag, f32[19,4,32,128]{3,2,1,0:T(8,128)S(1)} %get-tuple-element.19.cells, ...), custom_call_target="tpu_custom_call" | custom-call | tf_op jit(solution)/shard_map/finish/pallas_call | solution.py:807

commit v4 on v3

--- a/solution.py
+++ b/solution.py
@@ -363,6 +363,7 @@
     send_sem,
     recv_sem,
     drag_sem,
+    relay_sem,
 ):
     sx, sy, sz = mesh_sizes
     nx, ny, nz = extent
@@ -399,7 +400,7 @@
     faces = [tuple(s if d == dim else 0 for d in range(3)) for dim in range(3) for s in (1, -1)]
     edges = [
         tuple(s if d == p else t if d == q else 0 for d in range(3))
-        for p, q in ((0, 2), (1, 2), (0, 1))
+        for p, q in ((1, 2), (0, 2), (0, 1))
         for s in (1, -1)
         for t in (1, -1)
     ]
@@ -408,26 +409,44 @@
     near_part = [d for d in faces if not d[0]]
     side_part = [d for d in around if d[0]]
 
-    pair, core = me[0] // 2, me[0] % 2
     pairs = sx // 2
+    pair = sum(jnp.where(me[0] >= 2 * n, 1, 0) for n in range(1, pairs)) if pairs > 1 else 0
+    core = me[0] - 2 * pair
+
+    def ahead(index, count, size):
+        moved = index + count
+        return jnp.where(moved >= size, moved - size, moved) if count else index
+
     first_group = [(c, z) for c in range(2) for z in range(sz) if (c, z) != (0, 0)]
     second_group = [(h, y) for h in range(pairs) for y in range(sy) if (h, y) != (0, 0)]
 
     def first_partner(c, z):
-        return (pair * 2 + lax.rem(core + c, 2), me[1], lax.rem(me[2] + z, sz))
+        return (pair * 2 + ahead(core, c, 2), me[1], ahead(me[2], z, sz))
 
     def second_partner(h, y):
-        return (lax.rem(pair + h, pairs) * 2 + core, lax.rem(me[1] + y, sy), me[2])
+        return (ahead(pair, h, pairs) * 2 + core, ahead(me[1], y, sy), me[2])
 
     barrier = pltpu.get_barrier_semaphore()
-    far = [(z, 1, first_partner(c, z)) for c, z in first_group if (c, z) not in ((0, 1), (0, sz - 1))]
-    far = [(min(z, sz - z), n, target) for z, n, target in far]
-    for h, y in second_group:
-        if (h, y) not in ((0, 1), (0, sy - 1)):
-            far.append((2 * h + (min(y, sy - y) + 1) // 2, 2, second_partner(h, y)))
+    def ring(count, size):
+        return min(count % size, -count % size)
+
+    def first_hops(c, z):
+        return ring(z, sz)
+
+    def second_hops(h, y):
+        if y % 2 == 0:
+            return 2 * h + ring(y // 2, sy // 2)
+        return 1 + max(ring(y // 2, sy // 2), ring(y // 2 + 1, sy // 2))
+
+    first_near = [o for o in first_group if first_hops(*o) <= 3]
+    first_far = [o for o in first_group if first_hops(*o) > 3]
+    second_near = [o for o in second_group if second_hops(*o) <= 3]
+    second_far = [o for o in second_group if second_hops(*o) > 3]
+    signals = [(first_hops(*o), first_partner(*o)) for o in first_near if o not in ((0, 1), (0, sz - 1))]
+    signals += [(second_hops(*o), second_partner(*o)) for o in second_near if o not in ((0, 1), (0, sy - 1))]
     for offset in around:
-        far.append((2 * abs(offset[0]) + abs(offset[1]) + abs(offset[2]), 3, shifted(offset)))
-    targets = [entry[2] for entry in sorted(far, key=lambda entry: -entry[0])]
+        signals.append((2 * abs(offset[0]) + 1.5 * abs(offset[1]) + abs(offset[2]), shifted(offset)))
+    targets = [entry[1] for entry in sorted(signals, key=lambda entry: -entry[0])]
     for target in targets:
         pl.semaphore_signal(barrier, inc=1, device_id=target, device_id_type=MESH)
 
@@ -472,8 +491,20 @@
                     column = pltpu.roll(column, turn, 1) if turn else column
                     packed = column if packed is None else jnp.where(lane == h, column, packed)
                 xz_send[step, slot(p) * 2 + slot(q)] = packed
-                row = 0 if p == 1 else ny - 1
-                yz_send[step, slot(p) * 2 + slot(q)] = columns_send[step, slot(q), row : row + 1, :]
+
+    def pack_corners(step, cells):
+        for p in (1, -1):
+            row = BODY if p == 1 else BODY + ny - 1
+            for q in (1, -1):
+                i = member_at((0, p, q))
+                packed = None
+                for x in range(nx):
+                    spot = ALONG[2][q].index(i) * nx + x
+                    corner = cells[i, x, row : row + 1, :]
+                    turn = (spot if q == 1 else spot + 1) % nz
+                    corner = pltpu.roll(corner, turn, 1) if turn else corner
+                    packed = corner if packed is None else jnp.where(lane[0:1] == spot, corner, packed)
+                yz_send[step, slot(p) * 2 + slot(q)] = packed
 
     def message(step, direction):
         dx, dy, dz = direction
@@ -543,6 +574,7 @@
     loads[0].wait()
     pack(0, level_two, range(nx), False)
     pack_edges(0, level_two)
+    pack_corners(0, level_two)
     for load in loads[1:]:
         load.wait()
     total = jnp.zeros((8, nz), F32)
@@ -566,6 +598,8 @@
     pl.semaphore_wait(barrier, len(targets))
 
     send(0, around)
+    pl.semaphore_signal(relay_sem.at[0], inc=1, device_id=first_partner(0, sz - 2), device_id_type=MESH)
+    pl.semaphore_signal(relay_sem.at[1], inc=1, device_id=second_partner(1, 0), device_id_type=MESH)
     near_rows = sum(message_rows(d, extent) for d in near_part)
     side_rows = sum(message_rows(d, extent) for d in side_part)
     corner_rows = sum(message_rows(d, extent) for d in corner_part)
@@ -576,7 +610,6 @@
     drag_second = drag_slots.at[pl.ds(2 * sz, pairs * sy)]
 
     def drag_send(stage, target, mine, group, partner):
-        target[mine] = drag_row[stage]
         for offset in group:
             pltpu.make_async_remote_copy(
                 src_ref=drag_row.at[stage],
@@ -587,7 +620,8 @@
                 device_id_type=MESH,
             ).start()
 
-    drag_send(0, drag_first, mine_first, first_group, first_partner)
+    drag_first[mine_first] = drag_row[0]
+    drag_send(0, drag_first, mine_first, first_near, first_partner)
 
     for step, t in ((0, 1), (1, 0)):
         for x in range(nx):
@@ -610,15 +644,25 @@
             for i in range(19):
                 level_one[i, x, BODY + 8 * h : BODY + 8 * h + 8, :] = fresh[i]
                 sums[i, x, rows, :] = weighed[i]
-
-    def first_corners(x):
+            for sign, near in ((1, 0), (-1, nx - 1)):
+                if x == near:
+                    for k, i in enumerate(ALONG[0][sign]):
+                        face_send[1, slot(sign), k, rows, :] = fresh[i]
+
+    def first_corners(x, changes, members):
         for dy in (1, -1):
             h = corner_tile(extent, dy)[0]
-            change = corner_change(yz_recv[0], extent, dy, x)
-            for i in range(19):
+            for i in members:
                 rows = slice(BODY + 8 * h, BODY + 8 * h + 8)
-                level_one[i, x, rows, :] = level_one[i, x, rows, :] + change * response[0, slot(dy), i, x]
-
+                value = level_one[i, x, rows, :] + changes[x, dy] * response[0, slot(dy), i, x]
+                level_one[i, x, rows, :] = value
+                for sign, near in ((1, 0), (-1, nx - 1)):
+                    if x == near and i in ALONG[0][sign]:
+                        face_send[1, slot(sign), ALONG[0][sign].index(i), 8 * h : 8 * h + 8, :] = value
+
+    pl.semaphore_wait(relay_sem.at[0], 1)
+    pl.semaphore_wait(relay_sem.at[1], 1)
+    drag_send(0, drag_first, mine_first, first_far, first_partner)
     await_rows(near_rows, recv_sem.at[0, 0])
     insert_rows(0, level_two)
     for x in inner:
@@ -628,18 +672,26 @@
     for x in outer:
         first_level(x)
     await_rows(corner_rows, recv_sem.at[0, 2])
-    for x in outer + inner:
-        first_corners(x)
-    for sign, near in ((1, 0), (-1, nx - 1)):
-        for k, i in enumerate(ALONG[0][sign]):
-            face_send[1, slot(sign), k] = level_one[i, near, body, :]
+    changes = {(x, dy): corner_change(yz_recv[0], extent, dy, x) for x in range(nx) for dy in (1, -1)}
+    at_corner = tuple(member_at((0, p, q)) for p in (1, -1) for q in (1, -1))
+    elsewhere = tuple(i for i in range(19) if i not in at_corner)
+    for x in range(nx):
+        first_corners(x, changes, at_corner)
+    pack_corners(1, level_one)
+    send(1, corner_part)
+    for x in outer:
+        first_corners(x, changes, elsewhere)
+    pack_edges(1, level_one)
+    send(1, side_part)
+    for x in inner:
+        first_corners(x, changes, elsewhere)
     pack(1, level_one, range(nx), False)
-    pack_edges(1, level_one)
-    send(1, around)
+    send(1, near_part)
 
     await_rows(len(first_group), drag_sem.at[0])
     drag_row[1] = jnp.sum(drag_first[...], axis=0)
-    drag_send(1, drag_second, mine_second, second_group, second_partner)
+    drag_second[mine_second] = drag_row[1]
+    drag_send(1, drag_second, mine_second, second_far + second_near, second_partner)
 
     for x in range(nx):
         for h in range(halves):
@@ -799,6 +851,7 @@
                 pltpu.SemaphoreType.DMA((1,)),
                 pltpu.SemaphoreType.DMA((2, 3)),
                 pltpu.SemaphoreType.DMA((3,)),
+                pltpu.SemaphoreType.REGULAR((2,)),
             ],
             compiler_params=pltpu.CompilerParams(
                 collective_id=0, has_side_effects=True, vmem_limit_bytes=16 << 20

time: 22.8 us -> 22.4 us (0.982)
  Pallas kernels: 22 us -> 21.7 us
    pallas_call x1, Pallas kernels: 21 us -> 20.7 us  [body(): pl.pallas_call(functools.partial(kernel, sizes, (nx, ny, nz)), name='adjo...]
where the time goes in v4:
time: 22.4 us; the launch traced here: 22.3 us
  Pallas kernels  21.7 us (97%)
  between operations  0.64 us (3%)
    pallas_call x1, Pallas kernels, body(): pl.pallas_call(functools.partial(kernel, sizes, (nx, ny, nz)), name='adjo...  20.7 us
    pallas_call x1, Pallas kernels, body(): pl.pallas_call(functools.partial(finish, (nx, ny, nz)), name='finish', ou...  0.99 us

profile of v4, /device:TPU:1, one launch (start us, length us, event | category | flops | bytes accessed | tf_op | source)
XLA Modules:
  0.0 22.3 jit_solution(2377590058132819931)
XLA Ops:
  0.6 20.7 %adjoint_window.1 = (f32[19,2,16,128]{3,2,1,0:T(8,128)S(1)}, f32[4,16,128]{2,1,0:T(8,128)S(1)}, f32[8,128]{1,0:T(8,128)S(1)}, f32[19,4,32,128]{3,2,1,0:T(8,128)S...) custom-call(f32[2,19,4,16,128]{4,3,2,1,0:T(8,128)} %primal.1, ...), custom_call_target="tpu_custom_call" | custom-call | tf_op jit(solution)/shard_map/adjoint_window/pallas_call | solution.py:811
  21.3 1.0 %finish.1 = (f32[19,4,16,128]{3,2,1,0:T(8,128)}, f32[4,16,128]{2,1,0:T(8,128)}, f32[1,1]{1,0:T(1,128)}) custom-call(f32[19,2,16,128]{3,2,1,0:T(8,128)S(1)} %get-tuple-element.16.inner, f32[4,16,128]{2,1,0:T(8,128)S(1)} %get-tuple-element.17.grad, f32[8,128]{1,0:T(8,128)S(1)} %get-tuple-element.18.drag, f32[19,4,32,128]{3,2,1,0:T(8,128)S(1)} %get-tuple-element.19.cells, ...), custom_call_target="tpu_custom_call" | custom-call | tf_op jit(solution)/shard_map/finish/pallas_call | solution.py:860

commit v5 on v4

--- a/solution.py
+++ b/solution.py
@@ -597,7 +597,9 @@
 
     pl.semaphore_wait(barrier, len(targets))
 
-    send(0, around)
+    send(0, side_part)
+    send(0, corner_part)
+    send(0, near_part)
     pl.semaphore_signal(relay_sem.at[0], inc=1, device_id=first_partner(0, sz - 2), device_id_type=MESH)
     pl.semaphore_signal(relay_sem.at[1], inc=1, device_id=second_partner(1, 0), device_id_type=MESH)
     near_rows = sum(message_rows(d, extent) for d in near_part)
@@ -678,11 +680,11 @@
     for x in range(nx):
         first_corners(x, changes, at_corner)
     pack_corners(1, level_one)
-    send(1, corner_part)
     for x in outer:
         first_corners(x, changes, elsewhere)
     pack_edges(1, level_one)
     send(1, side_part)
+    send(1, corner_part)
     for x in inner:
         first_corners(x, changes, elsewhere)
     pack(1, level_one, range(nx), False)

time: 22.4 us -> 22.4 us (level)
  no operation moved by 1% of the time
where the time goes in v5:
time: 22.4 us; the launch traced here: 22.3 us
  Pallas kernels  21.6 us (96%)
  between operations  0.64 us (3%)
    pallas_call x1, Pallas kernels, body(): pl.pallas_call(functools.partial(kernel, sizes, (nx, ny, nz)), name='adjo...  20.7 us
    pallas_call x1, Pallas kernels, body(): pl.pallas_call(functools.partial(finish, (nx, ny, nz)), name='finish', ou...  0.99 us

profile of v5, /device:TPU:1, one launch (start us, length us, event | category | flops | bytes accessed | tf_op | source)
XLA Modules:
  0.0 22.3 jit_solution(14085894456097085556)
XLA Ops:
  0.6 20.7 %adjoint_window.1 = (f32[19,2,16,128]{3,2,1,0:T(8,128)S(1)}, f32[4,16,128]{2,1,0:T(8,128)S(1)}, f32[8,128]{1,0:T(8,128)S(1)}, f32[19,4,32,128]{3,2,1,0:T(8,128)S...) custom-call(f32[2,19,4,16,128]{4,3,2,1,0:T(8,128)} %primal.1, ...), custom_call_target="tpu_custom_call" | custom-call | tf_op jit(solution)/shard_map/adjoint_window/pallas_call | solution.py:813
  21.3 1.0 %finish.1 = (f32[19,4,16,128]{3,2,1,0:T(8,128)}, f32[4,16,128]{2,1,0:T(8,128)}, f32[1,1]{1,0:T(1,128)}) custom-call(f32[19,2,16,128]{3,2,1,0:T(8,128)S(1)} %get-tuple-element.16.inner, f32[4,16,128]{2,1,0:T(8,128)S(1)} %get-tuple-element.17.grad, f32[8,128]{1,0:T(8,128)S(1)} %get-tuple-element.18.drag, f32[19,4,32,128]{3,2,1,0:T(8,128)S(1)} %get-tuple-element.19.cells, ...), custom_call_target="tpu_custom_call" | custom-call | tf_op jit(solution)/shard_map/finish/pallas_call | solution.py:862

commit v6 on v5

--- a/solution.py
+++ b/solution.py
@@ -690,11 +690,6 @@
     pack(1, level_one, range(nx), False)
     send(1, near_part)
 
-    await_rows(len(first_group), drag_sem.at[0])
-    drag_row[1] = jnp.sum(drag_first[...], axis=0)
-    drag_second[mine_second] = drag_row[1]
-    drag_send(1, drag_second, mine_second, second_far + second_near, second_partner)
-
     for x in range(nx):
         for h in range(halves):
             rows = slice(8 * h, 8 * h + 8)
@@ -705,6 +700,11 @@
                     change = corner_change(yz_recv[0], extent, dy, x)
                     total = total + change * corner_weight(terms[0], extent, dy, x)
             out_grad[x, rows, :] = total
+
+    await_rows(len(first_group), drag_sem.at[0])
+    drag_row[1] = jnp.sum(drag_first[...], axis=0)
+    drag_second[mine_second] = drag_row[1]
+    drag_send(1, drag_second, mine_second, second_far + second_near, second_partner)
 
     def second_level(x):
         for h in range(halves):

time: 22.4 us -> 22.4 us (level)
  no operation moved by 1% of the time
where the time goes in v6:
time: 22.4 us; the launch traced here: 22.3 us
  Pallas kernels  21.6 us (96%)
  between operations  0.64 us (3%)
    pallas_call x1, Pallas kernels, body(): pl.pallas_call(functools.partial(kernel, sizes, (nx, ny, nz)), name='adjo...  20.7 us
    pallas_call x1, Pallas kernels, body(): pl.pallas_call(functools.partial(finish, (nx, ny, nz)), name='finish', ou...  0.99 us

profile of v6, /device:TPU:1, one launch (start us, length us, event | category | flops | bytes accessed | tf_op | source)
XLA Modules:
  0.0 22.3 jit_solution(17455240523677120170)
XLA Ops:
  0.6 20.7 %adjoint_window.1 = (f32[19,2,16,128]{3,2,1,0:T(8,128)S(1)}, f32[4,16,128]{2,1,0:T(8,128)S(1)}, f32[8,128]{1,0:T(8,128)S(1)}, f32[19,4,32,128]{3,2,1,0:T(8,128)S...) custom-call(f32[2,19,4,16,128]{4,3,2,1,0:T(8,128)} %primal.1, ...), custom_call_target="tpu_custom_call" | custom-call | tf_op jit(solution)/shard_map/adjoint_window/pallas_call | solution.py:813
  21.3 1.0 %finish.1 = (f32[19,4,16,128]{3,2,1,0:T(8,128)}, f32[4,16,128]{2,1,0:T(8,128)}, f32[1,1]{1,0:T(1,128)}) custom-call(f32[19,2,16,128]{3,2,1,0:T(8,128)S(1)} %get-tuple-element.16.inner, f32[4,16,128]{2,1,0:T(8,128)S(1)} %get-tuple-element.17.grad, f32[8,128]{1,0:T(8,128)S(1)} %get-tuple-element.18.drag, f32[19,4,32,128]{3,2,1,0:T(8,128)S(1)} %get-tuple-element.19.cells, ...), custom_call_target="tpu_custom_call" | custom-call | tf_op jit(solution)/shard_map/finish/pallas_call | solution.py:862
